TPU v7x, 512 devices: a whole 4x4x16 slice. The times are simulated.
512 devices in a mesh: space: 32 (over z, core), tm: 16 (over y, x).
Axes of the slice: x: 4, y: 4, z: 16, core: 2. Of those that a mesh axis runs over, the one named last changes fastest.
Arguments:
- snapshots: bfloat16 [65536, 16384], P('space', 'tm'), may hold values from -6 to 6
- basis: bfloat16 [65536, 256], P(('space', 'tm')), may hold values from -0.0234375 to 0.0234375
- lengths: int32 [16, 64], P('tm'), may hold values from 1 to 61, as said below
- owners: int32 [16, 64], P('tm'), may hold values from 0 to 31, as said below
Outputs:
- gram_out: bfloat16 [16, 32, 392, 392], P('tm', 'space')
- target_out: bfloat16 [16, 32, 392, 256], P('tm', 'space')
Inputs may be any that keep to these rules, and one draw needn't show every extreme that they name: Each row of lengths sums to 1024. The trajectories that one owner holds in one row have 62 snapshots together at most, and in every row some owner holds exactly 62. `owners`: in every row each space index owns exactly two trajectories.
All inputs are finite; a program needn't handle non-finite values.
Results may differ from a plain program's by a relative error of at most 0.0057.
Values may be sent and summed in bfloat16 or wider, within the bound.
No kernel may reach another device: no remote copies, remote signals or barrier semaphores. Data moves between devices by JAX's collectives and lax.ppermute only.
A program may use at most 64 MiB of HBM per device.

v0:
```python
import jax
import jax.numpy as jnp
import numpy as np
from jax import lax
from jax.sharding import PartitionSpec as P

QM = 16


def slot_plan(length_row, owner_row, owner_count, capacity, snap_count):
    traj_end = jnp.cumsum(length_row)
    starts = traj_end - length_row
    snap_index = jnp.arange(snap_count, dtype=jnp.int32)
    member = (
        (snap_index[:, None] >= starts[None, :]) & (snap_index[:, None] < traj_end[None, :])
    ).astype(jnp.int32)
    snap_start = jnp.sum(member * starts[None, :], axis=1)
    snap_end = jnp.sum(member * traj_end[None, :], axis=1)
    snap_owner = jnp.sum(member * owner_row[None, :], axis=1)
    traj_index = jnp.arange(length_row.shape[0], dtype=jnp.int32)
    same_owner = owner_row[:, None] == owner_row[None, :]
    earlier = traj_index[None, :] < traj_index[:, None]
    offset = jnp.sum(jnp.where(same_owner & earlier, length_row[None, :], 0), axis=1)
    slot_index = jnp.sum(member * offset[None, :], axis=1) + snap_index - snap_start
    has_next = (snap_index + 1 < snap_end).astype(jnp.int32)
    destination = snap_owner * capacity + slot_index
    source_rows = jnp.full((owner_count * capacity,), -1, jnp.int32).at[destination].set(snap_index)
    live_rows = jnp.zeros((owner_count * capacity,), jnp.int32).at[destination].set(has_next)
    return (source_rows, live_rows)


def library(coords, live_slots, weight_scale):
    first_mode, second_mode = np.triu_indices(QM)
    products = coords[:, first_mode] * coords[:, second_mode]
    library_rows = jnp.concatenate([coords, products], axis=1).astype(jnp.bfloat16)
    successor = jnp.concatenate(
        [coords[1:], jnp.zeros((1, coords.shape[1]), jnp.float32)], axis=0
    ).astype(jnp.bfloat16)
    weighted = library_rows * live_slots[:, None].astype(jnp.bfloat16)
    dims = (((0,), (0,)), ((), ()))
    gram_matrix = (
        lax.dot_general(weighted, library_rows, dims, preferred_element_type=jnp.float32)
        * weight_scale
    )
    targets = (
        lax.dot_general(weighted, successor, dims, preferred_element_type=jnp.float32)
        * weight_scale
    )
    return (gram_matrix.astype(jnp.bfloat16), targets.astype(jnp.bfloat16))


def on_device(snapshots, basis, lengths, owners):
    dims = (((0,), (0,)), ((), ()))
    snap_count = snapshots.shape[1]
    gathered = lax.all_gather(basis, "tm", axis=0, tiled=True)
    partial_value = lax.dot_general(snapshots, gathered, dims, preferred_element_type=jnp.float32)
    owner_count = lax.axis_size("space")
    capacity = 2 * snap_count // owner_count - 2
    source_rows, live_rows = slot_plan(lengths[0], owners[0], owner_count, capacity, snap_count)
    own_index = lax.axis_index("space")
    mine = lax.dynamic_slice_in_dim(source_rows, own_index * capacity, capacity)
    summed = lax.psum(partial_value, "space")
    packed = jnp.take(summed, jnp.maximum(mine, 0), axis=0) * (mine >= 0)[:, None].astype(
        jnp.float32
    )
    live_slots = lax.dynamic_slice_in_dim(live_rows, own_index * capacity, capacity)
    gram_matrix, targets = library(packed, live_slots, owner_count / snap_count)
    return (gram_matrix[None, None], targets[None, None])


def solution(mesh):
    placed = (P("space", "tm"), P(("space", "tm"), None), P("tm", None), P("tm", None))
    return jax.shard_map(
        on_device,
        mesh=mesh,
        in_specs=placed,
        out_specs=(P("tm", "space", None, None), P("tm", "space", None, None)),
        check_vma=False,
    )
```

profile of v0, /device:TPU:1, one launch (start us, length us, event | category | flops | bytes accessed | tf_op | source)
XLA Modules:
  0.0 301.7 jit_solution(7914927873324652971)
XLA Ops:
  7.2 0.0 all-gather.2.cloned.1.call-start
  7.2 0.7 all-gather.2.cloned.1.call-update
  7.9 0.0 all-reduce.3.cloned.1.call-start
  7.9 0.7 copy.20
  8.7 0.1 reduce-window.4
  8.8 0.1 reduce
  8.9 0.9 select_reduce_fusion.4
  9.8 0.7 fusion.17
  10.5 0.8 select_reduce_fusion
  11.4 4.3 %scatter_custom_fusion.1 = s32[1984]{0:T(1024)S(1)} fusion(s32[1024]{0:T(1024)S(1)} %bitcast.28, s32[1024]{0:T(1024)S(1)} %fusion.16, s32[]{:T(128)} %constant.22.clone.1), kind=kCustom, calls=%fused_computation.35 | custom fusion | bytes 7940 | tf_op jit(solution)/shard_map/scatter | solution.py:28
  15.7 4.3 %scatter_custom_fusion = s32[1984]{0:T(1024)S(1)} fusion(s32[1024]{0:T(1024)S(1)} %bitcast.29, s32[1024]{0:T(1024)S(1)} %iota.19, s32[]{:T(128)} %constant.21.clone.1), kind=kCustom, calls=%fused_computation.37 | custom fusion | bytes 7940 | tf_op jit(solution)/shard_map/scatter | solution.py:27
  20.0 0.0 copy-start.1
  20.1 0.0 copy-start
  20.1 52.9 %all-gather.2.cloned.1.call-done = bf16[2048,256]{1,0:T(8,128)(2,1)} async-done(((bf16[128,256]{1,0:T(8,128)(2,1)}), bf16[2048,256]{1,0:T(8,128)(2,1)}) %all-gather.2.cloned.1.call-update) | async-done | bytes 1048592 | tf_op jit(solution)/shard_map/all_gather | solution.py:55
  72.9 4.8 %fusion.22 = f32[1024,256]{1,0:T(8,128)} fusion(bf16[2048,1024]{1,0:T(8,128)(2,1)} %param.8, bf16[2048,256]{1,0:T(8,128)(2,1)} %all-gather.2.cloned.1.call-done), kind=kOutput, calls=%fused_computation.51 | convolution fusion | flops 1073741824 | bytes 6291456 | tf_op jit(solution)/shard_map/dot_general | solution.py:56
  77.7 0.0 all-reduce.3.cloned.1.call-update
  77.7 0.1 dynamic-slice_convert_fusion
  77.8 0.1 broadcast_compare_fusion
  77.9 0.0 copy-done.1
  77.9 0.0 copy-done
  77.9 211.2 %all-reduce.3.cloned.1.call-done = f32[1024,256]{1,0:T(8,128)} async-done(((f32[1024,256]{1,0:T(8,128)}), f32[1024,256]{1,0:T(8,128)}) %all-reduce.3.cloned.1.call-update) | async-done | bytes 1048592 | tf_op jit(solution)/shard_map/psum | solution.py:62
  289.2 1.9 gather_fusion
  291.0 0.1 fusion.21
  291.1 0.1 copy.21
  291.2 0.7 gather_fusion.2
  291.9 0.7 gather_fusion.1
  292.6 0.1 copy.23
  292.7 0.1 copy.24
  292.8 1.1 fusion.1
  293.9 1.0 fusion.3
  (9 shorter events, 0.1 us)
Async XLA Ops:
  7.2 65.8 %all-gather.2.cloned.1.call-start = ((), (), s32[]{:S(2)}) async-start(), calls=%async_computation | async-start | bytes 1114112 | tf_op jit(solution)/shard_map/all_gather | solution.py:55
  7.9 281.3 %all-reduce.3.cloned.1.call-start = ((), (), s32[]{:S(2)}) async-start(), calls=%async_computation.1 | async-start | bytes 2097152 | tf_op jit(solution)/shard_map/psum | solution.py:62
  20.0 57.8 %copy-start.1 = (s32[136]{0:T(256)S(1)}, s32[136]{0:T(256)}, u32[]{:S(2)}) copy-start(s32[136]{0:T(256)} %constant.68) | copy-start | bytes 1636
  20.1 57.8 %copy-start = (s32[136]{0:T(256)S(1)}, s32[136]{0:T(256)}, u32[]{:S(2)}) copy-start(s32[136]{0:T(256)} %constant.69) | copy-start | bytes 1636
Sparse Core Ops, SparseCore 0:
  11.0 61.8 all-gather.1
  77.8 211.2 all-reduce.2
where the time goes:
time: 302 us
  waiting for transfers between devices  265 us (88%)
  between operations  14.2 us (5%)
  local copies, waits for them, and re-layouts  12.9 us (4%)
  matrix products  6.86 us (2%)
    psum x1, waiting for transfers between devices, on_device(): summed = lax.psum(partial_value, 'space')  211 us
    all_gather x1, waiting for transfers between devices, on_device(): gathered = lax.all_gather(basis, 'tm', axis=0, tiled=True)  52.9 us
  transfers between devices with their start and end apart: 2, of which 2 were waited for; matrix products, arithmetic and copies ran while one was open for 4% of the time, Pallas kernels for 0%

commit v1 on v0

v1 whole, which is shorter than its diff:
```python
import jax
import jax.numpy as jnp
import numpy as np
from jax import lax
from jax.sharding import PartitionSpec as P

QM = 16
SLOTS = 64
f32 = jnp.float32
bf16 = jnp.bfloat16


def plan(length, owner, own, parity, snap_count, chips):
    t = length.shape[0]
    ti = lax.broadcasted_iota(jnp.int32, (t, t), 0)
    tj = lax.broadcasted_iota(jnp.int32, (t, t), 1)
    before = tj < ti
    starts = jnp.sum(jnp.where(before, length[None, :], 0), axis=1)
    same = owner[:, None] == owner[None, :]
    offset = jnp.sum(jnp.where(before & same, length[None, :], 0), axis=1)
    base = jnp.where(
        jnp.bitwise_and(owner, 1) == parity,
        (owner // 2) * SLOTS + offset - starts,
        -2 * snap_count,
    )
    snap = lax.broadcasted_iota(jnp.int32, (t, snap_count), 1)
    member = (snap >= starts[:, None]) & (snap < (starts + length)[:, None])
    shift = jnp.sum(jnp.where(member, base[:, None], 0), axis=0)
    target = shift + jnp.arange(snap_count, dtype=jnp.int32)
    mine = owner == own
    total = jnp.sum(jnp.where(mine, length, 0))
    slot = lax.broadcasted_iota(jnp.int32, (SLOTS, t), 0)
    last = jnp.any(mine[None, :] & (slot == (offset + length - 1)[None, :]), axis=1)
    live = (jnp.arange(SLOTS) < total) & ~last
    return target, live


def library(coords, live, weight_scale):
    first_mode, second_mode = np.triu_indices(QM)
    pick_a = (first_mode[None, :] == lax.broadcasted_iota(jnp.int32, (QM, 1), 0)).astype(f32)
    pick_b = (second_mode[None, :] == lax.broadcasted_iota(jnp.int32, (QM, 1), 0)).astype(f32)
    lead = coords[:, :QM]
    hi = lax.Precision.HIGHEST
    products = jnp.dot(lead, pick_a, precision=hi) * jnp.dot(lead, pick_b, precision=hi)
    rows = jnp.concatenate([coords, products], axis=1).astype(bf16)
    successor = jnp.concatenate([coords[1:], jnp.zeros((1, coords.shape[1]), f32)], axis=0).astype(bf16)
    weighted = rows * live[:, None].astype(bf16)
    dims = (((0,), (0,)), ((), ()))
    gram = lax.dot_general(weighted, rows, dims, preferred_element_type=f32) * weight_scale
    target = lax.dot_general(weighted, successor, dims, preferred_element_type=f32) * weight_scale
    return gram.astype(bf16), target.astype(bf16)


def on_device(snapshots, basis, lengths, owners):
    snap_count = snapshots.shape[1]
    devices = lax.axis_size("space")
    chips = devices // 2
    groups_tm = lax.axis_size("tm")
    own = lax.axis_index("space")
    parity = jnp.bitwise_and(own, 1)

    copies = jnp.broadcast_to(basis[None], (groups_tm,) + basis.shape)
    gathered = lax.all_to_all(copies, "tm", 0, 0, tiled=True).reshape(-1, basis.shape[1])
    target, live = plan(lengths[0], owners[0], own, parity, snap_count, chips)
    partial = lax.dot_general(snapshots, gathered, (((0,), (0,)), ((), ())), preferred_element_type=f32)

    swap = [(i, i ^ 1) for i in range(devices)]
    other = lax.ppermute(partial.astype(bf16), "space", swap)
    chip_sum = (partial + other.astype(f32)).astype(bf16)
    slot = lax.broadcasted_iota(jnp.int32, (chips * SLOTS, snap_count), 0)
    select = (slot == target[None, :]).astype(bf16)
    packed = jnp.dot(select, chip_sum, preferred_element_type=f32).astype(bf16)
    along_z = [[2 * z + c for z in range(chips)] for c in range(2)]
    parts = lax.all_to_all(
        packed.reshape(chips, SLOTS, -1), "space", 0, 0, axis_index_groups=along_z, tiled=True
    )
    coords = jnp.sum(parts.astype(f32), axis=0)
    gram, targets = library(coords, live, devices / snap_count)
    return gram[None, None], targets[None, None]


def solution(mesh):
    placed = (P("space", "tm"), P(("space", "tm"), None), P("tm", None), P("tm", None))
    return jax.shard_map(
        on_device,
        mesh=mesh,
        in_specs=placed,
        out_specs=(P("tm", "space", None, None), P("tm", "space", None, None)),
        check_vma=False,
    )
```

time: 302 us -> 83.8 us (0.28)
  the two profiles are of different devices: /device:TPU:1 before, /device:TPU:32 now
where the time goes in v1:
time: 83.8 us; the launch traced here: 83.4 us
  waiting for transfers between devices  46.4 us (55%)
  starting transfers between devices  24.2 us (29%)
  matrix products  7.58 us (9%)
  other arithmetic  2.53 us (3%)
  local copies, waits for them, and re-layouts  1.96 us (2%)
    all_to_all x1, waiting for transfers between devices, on_device(): lax.all_to_all(packed.reshape(chips, SLOTS, -1), 'space', 0, 0, axis_inde...  28.5 us
    all_to_all x1, waiting for transfers between devices, on_device(): lax.all_to_all(copies, 'tm', 0, 0, tiled=True).reshape(-1, basis.shape[1])  16.7 us
    all_to_all x1, starting transfers between devices, on_device(): lax.all_to_all(packed.reshape(chips, SLOTS, -1), 'space', 0, 0, axis_inde...  15.2 us
    all_to_all x1, starting transfers between devices, on_device(): lax.all_to_all(copies, 'tm', 0, 0, tiled=True).reshape(-1, basis.shape[1])  7.03 us
    dot_general x1, matrix products, on_device(): lax.dot_general(snapshots, gathered, (((0,), (0,)), ((), ())), preferred_...  3.5 us
    broadcast_in_dim x1, local copies, waits for them, and re-layouts, on_device(): copies = jnp.broadcast_to(basis[None], (groups_tm,) + basis.shape)  1.93 us
    ppermute x1, starting transfers between devices, on_device(): other = lax.ppermute(partial.astype(bf16), 'space', swap)  1.92 us
  transfers between devices with their start and end apart: 3, of which 3 were waited for; matrix products, arithmetic and copies ran while one was open for 3% of the time, Pallas kernels for 0%

profile of v1, /device:TPU:32, one launch (start us, length us, event | category | flops | bytes accessed | tf_op | source)
XLA Modules:
  0.0 83.4 jit_solution(1688912971240022634)
XLA Ops:
  0.6 1.9 %broadcast_in_dim.61 = bf16[16,128,256]{2,1,0:T(8,128)(2,1)} broadcast(bf16[128,256]{1,0:T(8,128)(2,1)} %param.7), dimensions={1,2} | broadcast | bytes 1114112 | tf_op jit(solution)/shard_map/broadcast_in_dim | solution.py:62
  2.6 7.0 %all-to-all-start = ((bf16[16,128,256]{2,1,0:T(8,128)(2,1)}), bf16[16,128,256]{2,1,0:T(8,128)(2,1)S(1)}, u32[]{:S(2)}, u32[]{:S(2)}) async-start(bf16[16,128,256]{2,1,0:T(8,128)(2,1)} %broadcast_in_dim.61), calls=%async_computation | async-start | bytes 2097152 | tf_op jit(solution)/shard_map/all_to_all | solution.py:63
  9.6 0.9 %select_reduce_fusion.1 = (s32[64]{0:T(128)S(1)}, s32[64]{0:T(128)S(1)}) fusion(s32[64]{0:T(128)} %bitcast.25, s32[64]{0:T(128)} %bitcast.26), kind=kLoop, calls=%fused_computation.25 | loop fusion | flops 28544 | bytes 1024 | tf_op jit(solution)/shard_map/reduce_sum | solution.py:20
  10.5 16.7 %all-to-all-done = bf16[16,128,256]{2,1,0:T(8,128)(2,1)S(1)} async-done(((bf16[16,128,256]{2,1,0:T(8,128)(2,1)}), bf16[16,128,256]{2,1,0:T(8,128)(2,1)S(1)}, u32[]{:S(2)}, u32[]{:S(2)}) %all-to-all-start) | async-done | bytes 1048608 | tf_op jit(solution)/shard_map/all_to_all | solution.py:63
  27.2 0.0 copy-start
  27.2 0.0 copy-start.1
  27.3 3.5 %fusion.28 = (bf16[1024,256]{1,0:T(8,128)(2,1)S(1)}, f32[1024,256]{1,0:T(8,128)S(1)}) fusion(bf16[2048,1024]{1,0:T(8,128)(2,1)} %param.6, bf16[2048,256]{1,0:T(8,128)(2,1)S(1)} %bitcast.24), kind=kOutput, calls=%fused_computation.55 | convolution fusion | flops 1074003968 | bytes 6815744 | tf_op jit(solution)/shard_map/dot_general | solution.py:65
  30.8 0.0 copy-start.3
  30.8 0.0 copy-start.2
  30.8 1.9 %collective-permute-start = (bf16[1024,256]{1,0:T(8,128)(2,1)S(1)}, bf16[1024,256]{1,0:T(8,128)(2,1)S(1)}, u32[]{:S(2)}, u32[]{:S(2)}) collective-permute-start(bf16[1024,256]{1,0:T(8,128)(2,1)S(1)} %get-tuple-element.7), channel_id=1, source_target_pairs={{0,16},{16,0},{32,48},{48,32},{64,80},{80,64},{96,112},{112,96},{1... | collective-permute-start | bytes 1572872 | tf_op jit(solution)/shard_map/ppermute | solution.py:68
  32.7 0.0 copy-done
  32.7 0.0 copy-done.1
  32.7 0.6 fusion.22
  33.4 0.1 select_reduce_fusion
  33.5 1.1 %collective-permute-done = bf16[1024,256]{1,0:T(8,128)(2,1)S(1)} collective-permute-done((bf16[1024,256]{1,0:T(8,128)(2,1)S(1)}, bf16[1024,256]{1,0:T(8,128)(2,1)S(1)}, u32[]{:S(2)}, u32[]{:S(2)}) %collective-permute-start) | collective-permute-done | bytes 524320 | tf_op jit(solution)/shard_map/ppermute | solution.py:68
  34.6 1.7 %fusion.2 = bf16[1024,256]{1,0:T(8,128)(2,1)} fusion(s32[1024]{0:T(1024)S(1)} %iota_add_fusion, f32[1024,256]{1,0:T(8,128)S(1)} %get-tuple-element.8, bf16[1024,256]{1,0:T(8,128)(2,1)S(1)} %collective-permute-done), kind=kOutput, calls=%fused_computation.4 | convolution fusion | flops 538968064 | bytes 2101248 | tf_op jit(solution)/shard_map/dot_general | solution.py:72
  36.2 15.2 %all-to-all-start.1 = ((bf16[16,64,256]{2,1,0:T(8,128)(2,1)}), bf16[16,64,256]{2,1,0:T(8,128)(2,1)S(1)}, u32[]{:S(2)}, u32[]{:S(2)}) async-start(bf16[16,64,256]{2,1,0:T(8,128)(2,1)} %bitcast.3), calls=%async_computation.1 | async-start | bytes 1048576 | tf_op jit(solution)/shard_map/all_to_all | solution.py:74
  51.5 0.1 fusion.16
  51.6 0.7 and_convert_fusion
  52.3 28.5 %all-to-all-done.1 = bf16[16,64,256]{2,1,0:T(8,128)(2,1)S(1)} async-done(((bf16[16,64,256]{2,1,0:T(8,128)(2,1)}), bf16[16,64,256]{2,1,0:T(8,128)(2,1)S(1)}, u32[]{:S(2)}, u32[]{:S(2)}) %all-to-all-start.1) | async-done | bytes 524320 | tf_op jit(solution)/shard_map/all_to_all | solution.py:74
  80.8 0.1 convert_reduce_fusion
  80.9 0.0 copy-done.3
  80.9 0.2 fusion.18
  81.1 0.0 copy-done.2
  81.1 0.2 fusion.7
  81.3 1.1 %fusion.4 = bf16[1,1,392,392]{3,2,1,0:T(8,128)(2,1)} fusion(bf16[64,136]{1,0:T(8,128)(2,1)S(1)} %fusion.7, bf16[64,256]{1,0:T(8,128)(2,1)S(1)} %convert.9, bf16[64]{0:T(256)(128)(2,1)S(1)} %and_convert_fusion), kind=kOutput, calls=%fused_computation.7 | convolution fusion | flops 20227200 | bytes 357632 | tf_op jit(solution)/shard_map/dot_general | solution.py:49
  82.4 1.0 %fusion.6 = bf16[1,1,392,256]{3,2,1,0:T(8,128)(2,1)} fusion(bf16[64,136]{1,0:T(8,128)(2,1)S(1)} %fusion.7, bf16[64,256]{1,0:T(8,128)(2,1)S(1)} %convert.9, bf16[63,256]{1,0:T(8,128)(2,1)S(1)} %slice.10, bf16[64]{0:T(256)(128)(2,1)S(1)} %and_convert_fusion), kind=kOutput, calls=%fused_computation.9 | convolution fusion | flops 13196288 | bytes 283264 | tf_op jit(solution)/shard_map/dot_general | solution.py:50
  (5 shorter events, 0.0 us)
Async XLA Ops:
  2.6 24.7 %all-to-all-start = ((bf16[16,128,256]{2,1,0:T(8,128)(2,1)}), bf16[16,128,256]{2,1,0:T(8,128)(2,1)S(1)}, u32[]{:S(2)}, u32[]{:S(2)}) async-start(bf16[16,128,256]{2,1,0:T(8,128)(2,1)} %broadcast_in_dim.61), calls=%async_computation | async-start | bytes 2097152 | tf_op jit(solution)/shard_map/all_to_all | solution.py:63
  27.2 5.5 %copy-start = (s32[1,64]{1,0:T(1,128)S(1)}, s32[1,64]{1,0:T(1,128)}, u32[]{:S(2)}) copy-start(s32[1,64]{1,0:T(1,128)} %param.9) | copy-start | bytes 772
  27.2 5.5 %copy-start.1 = (s32[1,64]{1,0:T(1,128)S(1)}, s32[1,64]{1,0:T(1,128)}, u32[]{:S(2)}) copy-start(s32[1,64]{1,0:T(1,128)} %param.8) | copy-start | bytes 772
  30.8 50.2 %copy-start.3 = (s32[136]{0:T(256)S(1)}, s32[136]{0:T(256)}, u32[]{:S(2)}) copy-start(s32[136]{0:T(256)} %constant.49) | copy-start | bytes 1636
  30.8 50.3 %copy-start.2 = (s32[136]{0:T(256)S(1)}, s32[136]{0:T(256)}, u32[]{:S(2)}) copy-start(s32[136]{0:T(256)} %constant.50) | copy-start | bytes 1636
  30.8 3.8 %collective-permute-start = (bf16[1024,256]{1,0:T(8,128)(2,1)S(1)}, bf16[1024,256]{1,0:T(8,128)(2,1)S(1)}, u32[]{:S(2)}, u32[]{:S(2)}) collective-permute-start(bf16[1024,256]{1,0:T(8,128)(2,1)S(1)} %get-tuple-element.7), channel_id=1, source_target_pairs={{0,16},{16,0},{32,48},{48,32},{64,80},{80,64},{96,112},{112,96},{1... | collective-permute-start | bytes 1572872 | tf_op jit(solution)/shard_map/ppermute | solution.py:68
  36.2 44.6 %all-to-all-start.1 = ((bf16[16,64,256]{2,1,0:T(8,128)(2,1)}), bf16[16,64,256]{2,1,0:T(8,128)(2,1)S(1)}, u32[]{:S(2)}, u32[]{:S(2)}) async-start(bf16[16,64,256]{2,1,0:T(8,128)(2,1)} %bitcast.3), calls=%async_computation.1 | async-start | bytes 1048576 | tf_op jit(solution)/shard_map/all_to_all | solution.py:74

commit v2 on v1

--- a/solution.py
+++ b/solution.py
@@ -18,9 +18,12 @@
     starts = jnp.sum(jnp.where(before, length[None, :], 0), axis=1)
     same = owner[:, None] == owner[None, :]
     offset = jnp.sum(jnp.where(before & same, length[None, :], 0), axis=1)
+    chip = jnp.right_shift(owner, 1)
+    other_parity = jnp.bitwise_and(chip + jnp.right_shift(own, 1), 1)
+    place = other_parity * (chips // 2) + jnp.right_shift(chip, 1)
     base = jnp.where(
         jnp.bitwise_and(owner, 1) == parity,
-        (owner // 2) * SLOTS + offset - starts,
+        place * SLOTS + offset - starts,
         -2 * snap_count,
     )
     snap = lax.broadcasted_iota(jnp.int32, (t, snap_count), 1)
@@ -62,17 +65,33 @@
     copies = jnp.broadcast_to(basis[None], (groups_tm,) + basis.shape)
     gathered = lax.all_to_all(copies, "tm", 0, 0, tiled=True).reshape(-1, basis.shape[1])
     target, live = plan(lengths[0], owners[0], own, parity, snap_count, chips)
-    partial = lax.dot_general(snapshots, gathered, (((0,), (0,)), ((), ())), preferred_element_type=f32)
-
     swap = [(i, i ^ 1) for i in range(devices)]
-    other = lax.ppermute(partial.astype(bf16), "space", swap)
-    chip_sum = (partial + other.astype(f32)).astype(bf16)
+    half = snap_count // 2
+    sums = []
+    for at in (0, half):
+        partial = lax.dot_general(
+            snapshots[:, at : at + half], gathered, (((0,), (0,)), ((), ())), preferred_element_type=f32
+        )
+        total = partial + lax.ppermute(partial, "space", swap)
+        high = lax.reduce_precision(total, 8, 7)
+        sums.append((high.astype(bf16), (total - high).astype(bf16)))
     slot = lax.broadcasted_iota(jnp.int32, (chips * SLOTS, snap_count), 0)
     select = (slot == target[None, :]).astype(bf16)
-    packed = jnp.dot(select, chip_sum, preferred_element_type=f32).astype(bf16)
-    along_z = [[2 * z + c for z in range(chips)] for c in range(2)]
+    dims = (((1,), (0,)), ((), ()))
+    rows = chips // 2 * SLOTS
+    keep, give = 0.0, 0.0
+    for i, (high, low) in enumerate(sums):
+        columns = select[:, i * half : (i + 1) * half]
+        keep = keep + lax.dot_general(columns[:rows], high, dims, preferred_element_type=f32)
+        keep = keep + lax.dot_general(columns[:rows], low, dims, preferred_element_type=f32)
+        give = give + lax.dot_general(columns[rows:], high, dims, preferred_element_type=f32)
+    give = give.astype(bf16)
+    pair = {0: lambda z: z ^ 1, 1: lambda z: ((z + 1) ^ 1) - 1}
+    pairs = [(2 * z + c, 2 * (pair[c](z) % chips) + c) for z in range(chips) for c in range(2)]
+    summed = (keep + lax.ppermute(give, "space", pairs).astype(f32)).astype(bf16)
+    along_z = [[2 * z + c for z in range(p, chips, 2)] for p in range(2) for c in range(2)]
     parts = lax.all_to_all(
-        packed.reshape(chips, SLOTS, -1), "space", 0, 0, axis_index_groups=along_z, tiled=True
+        summed.reshape(chips // 2, SLOTS, -1), "space", 0, 0, axis_index_groups=along_z, tiled=True
     )
     coords = jnp.sum(parts.astype(f32), axis=0)
     gram, targets = library(coords, live, devices / snap_count)

time: 83.8 us -> 87.1 us (1.039)
  the two profiles are of different devices: /device:TPU:32 before, /device:TPU:1 now
where the time goes in v2:
time: 87.1 us; the launch traced here: 86.7 us
  waiting for transfers between devices  36.4 us (42%)
  starting transfers between devices  34.9 us (40%)
  matrix products  8.36 us (10%)
  other arithmetic  4.13 us (5%)
  local copies, waits for them, and re-layouts  1.97 us (2%)
  between operations  0.89 us (1%)
    all_to_all x1, waiting for transfers between devices, on_device(): lax.all_to_all(summed.reshape(chips // 2, SLOTS, -1), 'space', 0, 0, axis...  20.2 us
    all_to_all x1, waiting for transfers between devices, on_device(): lax.all_to_all(copies, 'tm', 0, 0, tiled=True).reshape(-1, basis.shape[1])  12.1 us
    ppermute x1, starting transfers between devices, on_device(): lax.ppermute(give, 'space', pairs).astype(f32)  11.2 us
    all_to_all x1, starting transfers between devices, on_device(): lax.all_to_all(summed.reshape(chips // 2, SLOTS, -1), 'space', 0, 0, axis...  8.26 us
    ppermute x2, starting transfers between devices, on_device(): total = partial + lax.ppermute(partial, 'space', swap)  7.9 us
    all_to_all x1, starting transfers between devices, on_device(): lax.all_to_all(copies, 'tm', 0, 0, tiled=True).reshape(-1, basis.shape[1])  7.58 us
    dot_general x2, matrix products, on_device(): lax.dot_general(snapshots[:, at:at + half], gathered, (((0,), (0,)), ((),...  3.22 us
    ppermute x1, waiting for transfers between devices, on_device(): lax.ppermute(give, 'space', pairs).astype(f32)  3.01 us
  transfers between devices with their start and end apart: 5, of which 4 were waited for; matrix products, arithmetic and copies ran while one was open for 7% of the time, Pallas kernels for 0%

profile of v2, /device:TPU:1, one launch (start us, length us, event | category | flops | bytes accessed | tf_op | source)
XLA Modules:
  0.0 86.7 jit_solution(9299530368554305464)
XLA Ops:
  0.6 1.9 %broadcast_in_dim.63 = bf16[16,128,256]{2,1,0:T(8,128)(2,1)} broadcast(bf16[128,256]{1,0:T(8,128)(2,1)} %param.7), dimensions={1,2} | broadcast | bytes 1114112 | tf_op jit(solution)/shard_map/broadcast_in_dim | solution.py:65
  2.6 7.6 %all-to-all-start = ((bf16[16,128,256]{2,1,0:T(8,128)(2,1)}), bf16[16,128,256]{2,1,0:T(8,128)(2,1)S(1)}, u32[]{:S(2)}, u32[]{:S(2)}) async-start(bf16[16,128,256]{2,1,0:T(8,128)(2,1)} %broadcast_in_dim.63), calls=%async_computation | async-start | bytes 2097152 | tf_op jit(solution)/shard_map/all_to_all | solution.py:66
  10.2 0.9 %select_reduce_fusion.1 = (s32[64]{0:T(128)S(1)}, s32[64]{0:T(128)S(1)}) fusion(s32[64]{0:T(128)} %bitcast.30, s32[64]{0:T(128)} %bitcast.31), kind=kLoop, calls=%fused_computation.50 | loop fusion | flops 28544 | bytes 1024 | tf_op jit(solution)/shard_map/reduce_sum | solution.py:20
  11.1 1.3 %fusion.44 = (s32[]{:T(128)}, s32[64]{0:T(128)S(1)}, s32[64]{0:T(128)S(1)}) fusion(s32[]{:T(128)S(6)} %axis_index.15, s32[1,64]{1,0:T(1,128)} %param.9, s32[1,64]{1,0:T(1,128)} %param.8, s32[64]{0:T(128)S(1)} %get-tuple-element.3, s32[64]{0:T(128)S(1)} %get-tuple-element.2, s32[]{:T(128)S(6)} %shift_right_arithmetic.18, s32[]{:T(128)S(6)} %and.43), kind=kLoop, calls=%fused_computation.68 | loop fusion | flops 1023 | bytes 1552 | tf_op jit(solution)/shard_map/reduce_sum | solution.py:34
  12.4 0.1 select_reduce_fusion
  12.5 12.1 %all-to-all-done = bf16[16,128,256]{2,1,0:T(8,128)(2,1)S(1)} async-done(((bf16[16,128,256]{2,1,0:T(8,128)(2,1)}), bf16[16,128,256]{2,1,0:T(8,128)(2,1)S(1)}, u32[]{:S(2)}, u32[]{:S(2)}) %all-to-all-start) | async-done | bytes 1048608 | tf_op jit(solution)/shard_map/all_to_all | solution.py:66
  24.6 2.5 %fusion = f32[512,256]{1,0:T(8,128)S(1)} fusion(bf16[2048,256]{1,0:T(8,128)(2,1)S(1)} %bitcast.28, bf16[2048,1024]{1,0:T(8,128)(2,1)} %param.6), kind=kOutput, calls=%fused_computation.1 | convolution fusion | flops 536870912 | bytes 3670016 | tf_op jit(solution)/shard_map/dot_general | solution.py:72
  27.1 6.0 %collective-permute-start.1 = (f32[512,256]{1,0:T(8,128)S(1)}, f32[512,256]{1,0:T(8,128)S(1)}, u32[]{:S(2)}, u32[]{:S(2)}) collective-permute-start(f32[512,256]{1,0:T(8,128)S(1)} %fusion), channel_id=1, source_target_pairs={{0,16},{16,0},{32,48},{48,32},{64,80},{80,64},{96,112},{112,96},{1... | collective-permute-start | bytes 1572872 | tf_op jit(solution)/shard_map/ppermute | solution.py:75
  33.1 0.8 iota_compare_fusion
  33.9 0.7 fusion.2
  34.7 1.9 %collective-permute-start = (f32[512,256]{1,0:T(8,128)S(1)}, f32[512,256]{1,0:T(8,128)S(1)}, u32[]{:S(2)}, u32[]{:S(2)}) collective-permute-start(f32[512,256]{1,0:T(8,128)S(1)} %fusion.2), channel_id=1, source_target_pairs={{0,16},{16,0},{32,48},{48,32},{64,80},{80,64},{96,112},{112,96},{1... | collective-permute-start | bytes 1572872 | tf_op jit(solution)/shard_map/ppermute | solution.py:75
  36.6 0.1 reduce-precision_convert_fusion
  36.7 0.3 fusion.14
  37.0 0.3 fusion.19
  37.4 1.1 %collective-permute-done = f32[512,256]{1,0:T(8,128)S(1)} collective-permute-done((f32[512,256]{1,0:T(8,128)S(1)}, f32[512,256]{1,0:T(8,128)S(1)}, u32[]{:S(2)}, u32[]{:S(2)}) %collective-permute-start) | collective-permute-done | bytes 524320 | tf_op jit(solution)/shard_map/ppermute | solution.py:75
  38.5 0.1 reduce-precision_convert_fusion.1
  38.6 0.0 copy-start.3
  38.6 0.0 copy-start.2
  38.6 0.3 fusion.10
  38.9 11.2 %collective-permute-start.2 = (bf16[512,256]{1,0:T(8,128)(2,1)S(1)}, bf16[512,256]{1,0:T(8,128)(2,1)S(1)}, u32[]{:S(2)}, u32[]{:S(2)}) collective-permute-start(bf16[512,256]{1,0:T(8,128)(2,1)S(1)} %fusion.10), channel_id=1, source_target_pairs={{0,32},{16,496},{32,0},{48,80},{64,96},{80,48},{96,64},{112,144},{... | collective-permute-start | bytes 786440 | tf_op jit(solution)/shard_map/ppermute | solution.py:91
  50.1 0.4 fusion.21
  50.5 0.4 fusion.17
  50.9 3.0 %collective-permute-done.2 = bf16[512,256]{1,0:T(8,128)(2,1)S(1)} collective-permute-done((bf16[512,256]{1,0:T(8,128)(2,1)S(1)}, bf16[512,256]{1,0:T(8,128)(2,1)S(1)}, u32[]{:S(2)}, u32[]{:S(2)}) %collective-permute-start.2) | collective-permute-done | bytes 262176 | tf_op jit(solution)/shard_map/ppermute | solution.py:91
  53.9 1.0 %fusion.9 = bf16[512,256]{1,0:T(8,128)(2,1)} fusion(f32[512,256]{1,0:T(8,128)S(1)} %fusion.17, f32[512,256]{1,0:T(8,128)S(1)} %fusion.19, f32[512,256]{1,0:T(8,128)S(1)} %fusion.21, bf16[512,256]{1,0:T(8,128)(2,1)S(1)} %reduce-precision_convert_fusion.1, pred[1024,1024]{1,0:T(32,128)(4,1)S(1)} %iota_compare_fusion, ...), kind=kOutput, calls=%fused_computation.14 | convolution fusion | flops 135004160 | bytes 2621440 | tf_op jit(solution)/shard_map/dot_general | solution.py:85
  54.9 8.3 %all-to-all-start.1 = ((bf16[8,64,256]{2,1,0:T(8,128)(2,1)}), bf16[8,64,256]{2,1,0:T(8,128)(2,1)S(1)}, u32[]{:S(2)}, u32[]{:S(2)}) async-start(bf16[8,64,256]{2,1,0:T(8,128)(2,1)} %bitcast.3), calls=%async_computation.1 | async-start | bytes 524288 | tf_op jit(solution)/shard_map/all_to_all | solution.py:93
  63.2 0.1 fusion.38
  63.3 0.7 and_convert_fusion
  64.0 20.2 %all-to-all-done.1 = bf16[8,64,256]{2,1,0:T(8,128)(2,1)S(1)} async-done(((bf16[8,64,256]{2,1,0:T(8,128)(2,1)}), bf16[8,64,256]{2,1,0:T(8,128)(2,1)S(1)}, u32[]{:S(2)}, u32[]{:S(2)}) %all-to-all-start.1) | async-done | bytes 262176 | tf_op jit(solution)/shard_map/all_to_all | solution.py:93
  84.2 0.2 fusion.40
  84.4 0.2 fusion.13
  84.6 1.1 %fusion.8 = bf16[1,1,392,392]{3,2,1,0:T(8,128)(2,1)} fusion(bf16[64,136]{1,0:T(8,128)(2,1)S(1)} %fusion.13, bf16[64,256]{1,0:T(8,128)(2,1)S(1)} %convert.9, bf16[64]{0:T(256)(128)(2,1)S(1)} %and_convert_fusion), kind=kOutput, calls=%fused_computation.13 | convolution fusion | flops 20227200 | bytes 357632 | tf_op jit(solution)/shard_map/dot_general | solution.py:52
  85.7 1.0 %fusion.12 = bf16[1,1,392,256]{3,2,1,0:T(8,128)(2,1)} fusion(bf16[64,136]{1,0:T(8,128)(2,1)S(1)} %fusion.13, bf16[64,256]{1,0:T(8,128)(2,1)S(1)} %convert.9, bf16[63,256]{1,0:T(8,128)(2,1)S(1)} %slice.46, bf16[64]{0:T(256)(128)(2,1)S(1)} %and_convert_fusion), kind=kOutput, calls=%fused_computation.17 | convolution fusion | flops 13196288 | bytes 283264 | tf_op jit(solution)/shard_map/dot_general | solution.py:53
  (15 shorter events, 0.1 us)
Async XLA Ops:
  2.6 22.1 %all-to-all-start = ((bf16[16,128,256]{2,1,0:T(8,128)(2,1)}), bf16[16,128,256]{2,1,0:T(8,128)(2,1)S(1)}, u32[]{:S(2)}, u32[]{:S(2)}) async-start(bf16[16,128,256]{2,1,0:T(8,128)(2,1)} %broadcast_in_dim.63), calls=%async_computation | async-start | bytes 2097152 | tf_op jit(solution)/shard_map/all_to_all | solution.py:66
  24.6 9.3 %copy-start.4 = (bf16[2048,1024]{1,0:T(8,128)(2,1)S(1)}, bf16[2048,1024]{1,0:T(8,128)(2,1)}, u32[]{:S(2)}) copy-start(bf16[2048,1024]{1,0:T(8,128)(2,1)} %param.6) | copy-start | bytes 12582916
  27.1 9.5 %collective-permute-start.1 = (f32[512,256]{1,0:T(8,128)S(1)}, f32[512,256]{1,0:T(8,128)S(1)}, u32[]{:S(2)}, u32[]{:S(2)}) collective-permute-start(f32[512,256]{1,0:T(8,128)S(1)} %fusion), channel_id=1, source_target_pairs={{0,16},{16,0},{32,48},{48,32},{64,80},{80,64},{96,112},{112,96},{1... | collective-permute-start | bytes 1572872 | tf_op jit(solution)/shard_map/ppermute | solution.py:75
  34.7 3.8 %collective-permute-start = (f32[512,256]{1,0:T(8,128)S(1)}, f32[512,256]{1,0:T(8,128)S(1)}, u32[]{:S(2)}, u32[]{:S(2)}) collective-permute-start(f32[512,256]{1,0:T(8,128)S(1)} %fusion.2), channel_id=1, source_target_pairs={{0,16},{16,0},{32,48},{48,32},{64,80},{80,64},{96,112},{112,96},{1... | collective-permute-start | bytes 1572872 | tf_op jit(solution)/shard_map/ppermute | solution.py:75
  38.6 24.6 %copy-start = (s32[1,64]{1,0:T(1,128)S(1)}, s32[1,64]{1,0:T(1,128)}, u32[]{:S(2)}) copy-start(s32[1,64]{1,0:T(1,128)} %param.9) | copy-start | bytes 772
  38.6 24.6 %copy-start.1 = (s32[1,64]{1,0:T(1,128)S(1)}, s32[1,64]{1,0:T(1,128)}, u32[]{:S(2)}) copy-start(s32[1,64]{1,0:T(1,128)} %param.8) | copy-start | bytes 772
  38.6 45.6 %copy-start.3 = (s32[136]{0:T(256)S(1)}, s32[136]{0:T(256)}, u32[]{:S(2)}) copy-start(s32[136]{0:T(256)} %constant.40) | copy-start | bytes 1636
  38.6 45.8 %copy-start.2 = (s32[136]{0:T(256)S(1)}, s32[136]{0:T(256)}, u32[]{:S(2)}) copy-start(s32[136]{0:T(256)} %constant.41) | copy-start | bytes 1636
  38.9 14.9 %collective-permute-start.2 = (bf16[512,256]{1,0:T(8,128)(2,1)S(1)}, bf16[512,256]{1,0:T(8,128)(2,1)S(1)}, u32[]{:S(2)}, u32[]{:S(2)}) collective-permute-start(bf16[512,256]{1,0:T(8,128)(2,1)S(1)} %fusion.10), channel_id=1, source_target_pairs={{0,32},{16,496},{32,0},{48,80},{64,96},{80,48},{96,64},{112,144},{... | collective-permute-start | bytes 786440 | tf_op jit(solution)/shard_map/ppermute | solution.py:91
  54.9 29.2 %all-to-all-start.1 = ((bf16[8,64,256]{2,1,0:T(8,128)(2,1)}), bf16[8,64,256]{2,1,0:T(8,128)(2,1)S(1)}, u32[]{:S(2)}, u32[]{:S(2)}) async-start(bf16[8,64,256]{2,1,0:T(8,128)(2,1)} %bitcast.3), calls=%async_computation.1 | async-start | bytes 524288 | tf_op jit(solution)/shard_map/all_to_all | solution.py:93

commit v3 on v1

v3 whole, which is shorter than its diff:
```python
import jax
import jax.numpy as jnp
import numpy as np
from jax import lax
from jax.experimental import pallas as pl
from jax.experimental.pallas import tpu as pltpu
from jax.sharding import PartitionSpec as P

QM = 16
SLOTS = 64
LANES = 128
f32 = jnp.float32
bf16 = jnp.bfloat16
i32 = jnp.int32
VMEM = pl.BlockSpec(memory_space=pltpu.VMEM)
SMEM = pl.BlockSpec(memory_space=pltpu.SMEM)


def iota(shape, axis):
    return lax.broadcasted_iota(i32, shape, axis)


def prepare_kernel(own_ref, length_ref, owner_ref, select_ref, live_ref):
    own = own_ref[0]
    t = length_ref.shape[1]
    snap_count = select_ref.shape[1]
    ti, tj = iota((t, t), 0), iota((t, t), 1)
    length_row = jnp.broadcast_to(length_ref[...], (t, t))
    owner_row = jnp.broadcast_to(owner_ref[...], (t, t))
    length_col = jnp.sum(jnp.where(ti == tj, length_row, 0), axis=1, keepdims=True)
    owner_col = jnp.sum(jnp.where(ti == tj, owner_row, 0), axis=1, keepdims=True)
    same = owner_row == owner_col
    starts = jnp.sum(jnp.where(tj < ti, length_row, 0), axis=1, keepdims=True)
    offset = jnp.sum(jnp.where((tj < ti) & same, length_row, 0), axis=1, keepdims=True)
    base = jnp.where(
        jnp.bitwise_and(owner_col, 1) == jnp.bitwise_and(own, 1),
        jnp.right_shift(owner_col, 1) * SLOTS + offset - starts,
        -2 * snap_count,
    )
    snap = iota((t, snap_count), 1)
    member = (snap >= starts) & (snap < starts + length_col)
    target = jnp.sum(jnp.where(member, base, 0), axis=0, keepdims=True) + iota((1, snap_count), 1)
    for at in range(0, select_ref.shape[0], SLOTS):
        slot = iota((SLOTS, snap_count), 0) + at
        select_ref[pl.ds(at, SLOTS), :] = jnp.where(slot == target, 1.0, 0.0).astype(bf16)
    row = slice(0, 1)
    offset_row = jnp.sum(jnp.where((ti < tj) & same, length_col, 0), axis=0, keepdims=True)
    mine = owner_row[row] == own
    total = jnp.sum(jnp.where(mine, length_row[row], 0), axis=1, keepdims=True)
    here = iota((SLOTS, t), 0)
    ends = mine & (here == offset_row + length_row[row] - 1)
    last = jnp.sum(jnp.where(ends, 1, 0), axis=1, keepdims=True)
    live = (iota((SLOTS, 1), 0) < total) & (last == 0)
    live_ref[...] = jnp.broadcast_to(jnp.where(live, 1.0, 0.0), (SLOTS, LANES))


def spread_kernel(basis_ref, copies_ref, done):
    count = copies_ref.shape[0]
    moves = [pltpu.make_async_copy(basis_ref, copies_ref.at[i], done.at[i]) for i in range(count)]
    for move in moves:
        move.start()
    for move in moves:
        move.wait()


def spread(basis, count):
    return pl.pallas_call(
        spread_kernel,
        out_shape=jax.ShapeDtypeStruct((count,) + basis.shape, basis.dtype),
        in_specs=[VMEM],
        out_specs=pl.BlockSpec(memory_space=pl.ANY),
        scratch_shapes=[pltpu.SemaphoreType.DMA((count,))],
        name="spread",
    )(basis)


def project_kernel(snapshots_ref, basis_ref, partial_ref, sent_ref):
    piece = lax.dot_general(
        basis_ref[...], snapshots_ref[...], (((0,), (0,)), ((), ())), preferred_element_type=f32
    )
    partial_ref[...] = piece
    sent_ref[...] = piece.astype(bf16)


def project(snapshots, basis, step):
    cells, snap_count = snapshots.shape
    modes = basis.shape[1]
    piece = pl.BlockSpec((modes, step), lambda i: (0, i))
    return pl.pallas_call(
        project_kernel,
        grid=(snap_count // step,),
        out_shape=tuple(jax.ShapeDtypeStruct((modes, snap_count), kind) for kind in (f32, bf16)),
        in_specs=[pl.BlockSpec((cells, step), lambda i: (0, i)), VMEM],
        out_specs=(piece, piece),
        compiler_params=pltpu.CompilerParams(vmem_limit_bytes=50 << 20),
        cost_estimate=pl.CostEstimate(
            flops=2 * cells * snap_count * modes, bytes_accessed=2 * cells * snap_count, transcendentals=0
        ),
        name="project",
    )(snapshots, basis)


def pack_kernel(select_ref, partial_ref, other_ref, packed_ref):
    chip_sum = (partial_ref[...] + other_ref[...].astype(f32)).astype(bf16)
    step = 256
    for at in range(0, select_ref.shape[0], step):
        packed_ref[pl.ds(at, step), :] = lax.dot_general(
            select_ref[pl.ds(at, step), :], chip_sum, (((1,), (1,)), ((), ())), preferred_element_type=f32
        ).astype(bf16)


def library_kernel(weight_scale, parts_ref, live_ref, pick_ref, gram_ref, target_ref):
    coords = jnp.sum(parts_ref[...].astype(f32), axis=0)
    modes = coords.shape[1]
    terms = pick_ref.shape[1] // 2
    both = jnp.dot(
        coords[:, :LANES], pick_ref[...], precision=lax.Precision.HIGHEST, preferred_element_type=f32
    )
    products = both[:, :terms] * both[:, terms:]
    theta = jnp.concatenate([coords, products], axis=1).astype(bf16)[:, : gram_ref.shape[0]]
    live = live_ref[:, :1].astype(bf16)
    weighted = theta * live
    row = iota((SLOTS, modes), 0)
    successor = jnp.where(row < SLOTS - 1, pltpu.roll(coords, SLOTS - 1, 0), 0.0).astype(bf16)
    dims = (((0,), (0,)), ((), ()))
    gram = lax.dot_general(weighted, theta, dims, preferred_element_type=f32) * weight_scale
    gram_ref[...] = gram.astype(bf16)
    target = lax.dot_general(weighted, successor, dims, preferred_element_type=f32) * weight_scale
    target_ref[...] = target.astype(bf16)


def call(kernel, name, outs, specs, flops, nbytes, mib=24, **more):
    return pl.pallas_call(
        kernel,
        out_shape=outs,
        in_specs=specs,
        out_specs=jax.tree.map(lambda _: VMEM, outs),
        compiler_params=pltpu.CompilerParams(vmem_limit_bytes=mib << 20),
        cost_estimate=pl.CostEstimate(flops=flops, bytes_accessed=nbytes, transcendentals=0),
        name=name,
        **more,
    )


def picks():
    first_mode, second_mode = np.triu_indices(QM)
    table = np.zeros((LANES, 4 * LANES), np.float32)
    for term, (a, b) in enumerate(zip(first_mode, second_mode)):
        table[a, term] = 1.0
        table[b, 2 * LANES + term] = 1.0
    return len(first_mode), table


def on_device(snapshots, basis, lengths, owners):
    cells, snap_count = snapshots.shape
    modes = basis.shape[1]
    devices = lax.axis_size("space")
    chips = devices // 2
    groups_tm = lax.axis_size("tm")
    own = lax.axis_index("space")
    rows = chips * SLOTS
    shape = jax.ShapeDtypeStruct

    gathered = lax.all_to_all(spread(basis, groups_tm), "tm", 0, 0, tiled=True).reshape(-1, modes)
    select, live = call(
        prepare_kernel,
        "prepare",
        (shape((rows, snap_count), bf16), shape((SLOTS, LANES), f32)),
        [SMEM, VMEM, VMEM],
        4 * rows * snap_count,
        2 * rows * snap_count,
    )(own.reshape(1), lengths, owners)
    gathered, select = lax.optimization_barrier((gathered, select))
    partial, sent = project(snapshots, gathered, 256)
    swap = [(i, i ^ 1) for i in range(devices)]
    other = lax.ppermute(sent, "space", swap)
    packed = call(
        pack_kernel,
        "pack",
        shape((rows, modes), bf16),
        [VMEM, VMEM, VMEM],
        2 * rows * snap_count * modes,
        6 * snap_count * modes,
    )(select, partial, other)
    along_z = [[2 * z + c for z in range(chips)] for c in range(2)]
    parts = lax.all_to_all(
        packed.reshape(chips, SLOTS, -1), "space", 0, 0, axis_index_groups=along_z, tiled=True
    )
    term_count, table = picks()
    terms = modes + term_count
    gram, target = call(
        lambda *refs: library_kernel(devices / snap_count, *refs),
        "library",
        (shape((terms, terms), bf16), shape((terms, modes), bf16)),
        [VMEM, VMEM, VMEM],
        2 * SLOTS * terms * (terms + modes),
        2 * terms * (terms + modes),
    )(parts, live, jnp.asarray(table))
    return gram[None, None], target[None, None]


def solution(mesh):
    placed = (P("space", "tm"), P(("space", "tm"), None), P("tm", None), P("tm", None))
    return jax.shard_map(
        on_device,
        mesh=mesh,
        in_specs=placed,
        out_specs=(P("tm", "space", None, None), P("tm", "space", None, None)),
        check_vma=False,
    )
```

time: 83.8 us -> 81.9 us (0.977)
  blocking collectives: 0 us -> 44.2 us
  waiting for transfers between devices: 46.4 us -> 17.5 us
  starting transfers between devices: 24.2 us -> 8.97 us
  Pallas kernels: 0 us -> 8.94 us
  matrix products: 7.58 us -> 0 us
  other arithmetic: 2.53 us -> 0 us
    all_to_all x0 -> x1, blocking collectives: none -> 44.2 us  [on_device(): lax.all_to_all(packed.reshape(chips, SLOTS, -1), 'space', 0, 0, axis_inde...]
    all_to_all x2 -> x1, waiting for transfers between devices: 45.3 us -> 15.6 us  [on_device(): lax.all_to_all(spread(basis, groups_tm), 'tm', 0, 0, tiled=True)]
    all_to_all x2 -> x1, starting transfers between devices: 22.2 us -> 7.05 us  [on_device(): lax.all_to_all(spread(basis, groups_tm), 'tm', 0, 0, tiled=True)]
    pallas_call x0 -> x5, Pallas kernels: none -> 8.94 us  [the longest x1 4.13 us: project(): pl.pallas_call(project_kernel, grid=(snap_count // step,), out_shape=tupl...]
    dot_general x6 -> x0, matrix products: 7.58 us -> none  [the longest x1 3.5 us: on_device(): lax.dot_general(snapshots, gathered, (((0,), (0,)), ((), ())), preferred_...]
    broadcast_in_dim x1 -> x0, local copies, waits for them, and re-layouts: 1.93 us -> none  [on_device(): copies = jnp.broadcast_to(basis[None], (groups_tm,) + basis.shape)]
    reduce_sum x4 -> x0, other arithmetic: 1.74 us -> none  [the longest x1 0.91 us: plan(): offset = jnp.sum(jnp.where(before & same, length[None, :], 0), axis=1)]
    unnamed x8 -> x6, local copies, waits for them, and re-layouts: 0.02 us -> 1.31 us
  transfers between devices with their start and end apart: 3 -> 2, of which waited for: 3 -> 2; matrix products, arithmetic and copies ran while one was open for 3% -> 0% of each run, Pallas kernels for 0% -> 1%
where the time goes in v3:
time: 81.9 us; the launch traced here: 81.6 us
  blocking collectives  44.2 us (54%)
  waiting for transfers between devices  17.5 us (21%)
  starting transfers between devices  8.97 us (11%)
  Pallas kernels  8.94 us (11%)
  local copies, waits for them, and re-layouts  1.31 us (2%)
    all_to_all x1, blocking collectives, on_device(): lax.all_to_all(packed.reshape(chips, SLOTS, -1), 'space', 0, 0, axis_inde...  44.2 us
    all_to_all x1, waiting for transfers between devices, on_device(): lax.all_to_all(spread(basis, groups_tm), 'tm', 0, 0, tiled=True)  15.6 us
    all_to_all x1, starting transfers between devices, on_device(): lax.all_to_all(spread(basis, groups_tm), 'tm', 0, 0, tiled=True)  7.05 us
    pallas_call x1, Pallas kernels, project(): pl.pallas_call(project_kernel, grid=(snap_count // step,), out_shape=tupl...  4.13 us
    pallas_call x1, Pallas kernels, spread(): pl.pallas_call(spread_kernel, out_shape=jax.ShapeDtypeStruct((count,) + b...  1.95 us
    ppermute x1, starting transfers between devices, on_device(): other = lax.ppermute(sent, 'space', swap)  1.92 us
    ppermute x1, waiting for transfers between devices, on_device(): other = lax.ppermute(sent, 'space', swap)  1.88 us
  transfers between devices with their start and end apart: 2, of which 2 were waited for; matrix products, arithmetic and copies ran while one was open for 0% of the time, Pallas kernels for 1%

profile of v3, /device:TPU:32, one launch (start us, length us, event | category | flops | bytes accessed | tf_op | source)
XLA Modules:
  0.0 81.6 jit_solution(15050209898638802096)
XLA Ops:
  0.6 1.9 %spread.1 = bf16[16,128,256]{2,1,0:T(8,128)(2,1)} custom-call(bf16[128,256]{1,0:T(8,128)(2,1)} %basis_ref.1), custom_call_target="tpu_custom_call" | custom-call | tf_op jit(solution)/shard_map/spread/pallas_call | solution.py:67
  2.6 7.0 %all-to-all-start = ((bf16[16,128,256]{2,1,0:T(8,128)(2,1)}), bf16[16,128,256]{2,1,0:T(8,128)(2,1)S(1)}, u32[]{:S(2)}, u32[]{:S(2)}) async-start(bf16[16,128,256]{2,1,0:T(8,128)(2,1)} %spread.1), calls=%async_computation | async-start | bytes 2097152 | tf_op jit(solution)/shard_map/all_to_all | solution.py:164
  9.6 0.0 copy-start.1
  9.7 0.6 copy-done.1
  10.3 0.0 copy-start.2
  10.3 0.7 copy-done.2
  11.0 0.7 prepare.1
  11.7 15.6 %all-to-all-done = bf16[16,128,256]{2,1,0:T(8,128)(2,1)S(1)} async-done(((bf16[16,128,256]{2,1,0:T(8,128)(2,1)}), bf16[16,128,256]{2,1,0:T(8,128)(2,1)S(1)}, u32[]{:S(2)}, u32[]{:S(2)}) %all-to-all-start) | async-done | bytes 1048608 | tf_op jit(solution)/shard_map/all_to_all | solution.py:164
  27.3 0.0 copy-start
  27.3 4.1 %project.1 = (f32[256,1024]{1,0:T(8,128)S(1)}, bf16[256,1024]{1,0:T(8,128)(2,1)S(1)}) custom-call(bf16[2048,1024]{1,0:T(8,128)(2,1)} %snapshots_ref.1, bf16[2048,256]{1,0:T(8,128)(2,1)S(1)} %bitcast.5), custom_call_target="tpu_custom_call" | custom-call | flops 1073741824 | bytes 4194304 | tf_op jit(solution)/shard_map/project/pallas_call | solution.py:89
  31.4 1.9 %collective-permute-start = (bf16[256,1024]{1,0:T(8,128)(2,1)S(1)}, bf16[256,1024]{1,0:T(8,128)(2,1)S(1)}, u32[]{:S(2)}, u32[]{:S(2)}) collective-permute-start(bf16[256,1024]{1,0:T(8,128)(2,1)S(1)} %get-tuple-element.14), channel_id=1, source_target_pairs={{0,16},{16,0},{32,48},{48,32},{64,80},{80,64},{96,112},{112,96},{1... | collective-permute-start | bytes 1572872 | tf_op jit(solution)/shard_map/ppermute | solution.py:176
  33.3 1.9 %collective-permute-done.other_ref = bf16[256,1024]{1,0:T(8,128)(2,1)S(1)} collective-permute-done((bf16[256,1024]{1,0:T(8,128)(2,1)S(1)}, bf16[256,1024]{1,0:T(8,128)(2,1)S(1)}, u32[]{:S(2)}, u32[]{:S(2)}) %collective-permute-start) | collective-permute-done | bytes 524320 | tf_op jit(solution)/shard_map/ppermute | solution.py:176
  35.2 0.8 pack.1
  36.0 44.2 %all_to_all.10.refs_0_ = bf16[16,64,256]{2,1,0:T(8,128)(2,1)S(1)} all-to-all(bf16[16,64,256]{2,1,0:T(8,128)(2,1)S(1)} %bitcast.6), channel_id=1, replica_groups={{0,32,64,96,128,160,192,224,256,288,320,352,384,416,448,480},{16,48,80,..., dimensions={0} | all-to-all | bytes 1048576 | tf_op jit(solution)/shard_map/all_to_all | solution.py:186
  80.2 0.0 copy-done
  80.2 1.4 %library.1 = (bf16[392,392]{1,0:T(8,128)(2,1)}, bf16[392,256]{1,0:T(8,128)(2,1)}) custom-call(bf16[16,64,256]{2,1,0:T(8,128)(2,1)S(1)} %all_to_all.10.refs_0_, f32[64,128]{1,0:T(8,128)S(1)} %get-tuple-element.15.refs_1_, f32[128,512]{1,0:T(8,128)S(1)} %copy-done), custom_call_target="tpu_custom_call" | custom-call | flops 32514048 | bytes 508032 | tf_op jit(solution)/shard_map/library/pallas_call | solution.py:191
Async XLA Ops:
  2.6 24.7 %all-to-all-start = ((bf16[16,128,256]{2,1,0:T(8,128)(2,1)}), bf16[16,128,256]{2,1,0:T(8,128)(2,1)S(1)}, u32[]{:S(2)}, u32[]{:S(2)}) async-start(bf16[16,128,256]{2,1,0:T(8,128)(2,1)} %spread.1), calls=%async_computation | async-start | bytes 2097152 | tf_op jit(solution)/shard_map/all_to_all | solution.py:164
  9.6 0.7 copy-start.1
  10.3 0.7 copy-start.2
  27.3 52.9 %copy-start = (f32[128,512]{1,0:T(8,128)S(1)}, f32[128,512]{1,0:T(8,128)}, u32[]{:S(2)}) copy-start(f32[128,512]{1,0:T(8,128)} %constant.8.clone.refs_2_) | copy-start | bytes 786436
  31.4 3.8 %collective-permute-start = (bf16[256,1024]{1,0:T(8,128)(2,1)S(1)}, bf16[256,1024]{1,0:T(8,128)(2,1)S(1)}, u32[]{:S(2)}, u32[]{:S(2)}) collective-permute-start(bf16[256,1024]{1,0:T(8,128)(2,1)S(1)} %get-tuple-element.14), channel_id=1, source_target_pairs={{0,16},{16,0},{32,48},{48,32},{64,80},{80,64},{96,112},{112,96},{1... | collective-permute-start | bytes 1572872 | tf_op jit(solution)/shard_map/ppermute | solution.py:176

commit v4 on v3

--- a/solution.py
+++ b/solution.py
@@ -54,44 +54,35 @@
     live_ref[...] = jnp.broadcast_to(jnp.where(live, 1.0, 0.0), (SLOTS, LANES))
 
 
-def spread_kernel(basis_ref, copies_ref, done):
-    count = copies_ref.shape[0]
-    moves = [pltpu.make_async_copy(basis_ref, copies_ref.at[i], done.at[i]) for i in range(count)]
-    for move in moves:
-        move.start()
-    for move in moves:
-        move.wait()
-
-
-def spread(basis, count):
-    return pl.pallas_call(
-        spread_kernel,
-        out_shape=jax.ShapeDtypeStruct((count,) + basis.shape, basis.dtype),
-        in_specs=[VMEM],
-        out_specs=pl.BlockSpec(memory_space=pl.ANY),
-        scratch_shapes=[pltpu.SemaphoreType.DMA((count,))],
-        name="spread",
-    )(basis)
-
-
 def project_kernel(snapshots_ref, basis_ref, partial_ref, sent_ref):
-    piece = lax.dot_general(
-        basis_ref[...], snapshots_ref[...], (((0,), (0,)), ((), ())), preferred_element_type=f32
-    )
-    partial_ref[...] = piece
-    sent_ref[...] = piece.astype(bf16)
-
-
-def project(snapshots, basis, step):
+    left = jnp.concatenate([basis_ref[i] for i in range(basis_ref.shape[0])], axis=1)
+    piece = jnp.dot(left, snapshots_ref[...], preferred_element_type=f32)
+    step = pl.program_id(0)
+
+    @pl.when(step == 0)
+    def _():
+        partial_ref[...] = piece
+
+    @pl.when(step > 0)
+    def _():
+        total = partial_ref[...] + piece
+        partial_ref[...] = total
+        sent_ref[...] = total.astype(bf16)
+
+
+def project(snapshots, basis, steps):
     cells, snap_count = snapshots.shape
-    modes = basis.shape[1]
-    piece = pl.BlockSpec((modes, step), lambda i: (0, i))
+    blocks, modes, width = basis.shape
+    whole = pl.BlockSpec((modes, snap_count), lambda i: (0, 0))
     return pl.pallas_call(
         project_kernel,
-        grid=(snap_count // step,),
+        grid=(steps,),
         out_shape=tuple(jax.ShapeDtypeStruct((modes, snap_count), kind) for kind in (f32, bf16)),
-        in_specs=[pl.BlockSpec((cells, step), lambda i: (0, i)), VMEM],
-        out_specs=(piece, piece),
+        in_specs=[
+            pl.BlockSpec((cells // steps, snap_count), lambda i: (i, 0)),
+            pl.BlockSpec((blocks // steps, modes, width), lambda i: (i, 0, 0)),
+        ],
+        out_specs=(whole, whole),
         compiler_params=pltpu.CompilerParams(vmem_limit_bytes=50 << 20),
         cost_estimate=pl.CostEstimate(
             flops=2 * cells * snap_count * modes, bytes_accessed=2 * cells * snap_count, transcendentals=0
@@ -161,7 +152,8 @@
     rows = chips * SLOTS
     shape = jax.ShapeDtypeStruct
 
-    gathered = lax.all_to_all(spread(basis, groups_tm), "tm", 0, 0, tiled=True).reshape(-1, modes)
+    copies = jnp.broadcast_to(basis.T[None], (groups_tm, modes, basis.shape[0]))
+    gathered = lax.all_to_all(copies, "tm", 0, 0, tiled=True)
     select, live = call(
         prepare_kernel,
         "prepare",
@@ -170,8 +162,7 @@
         4 * rows * snap_count,
         2 * rows * snap_count,
     )(own.reshape(1), lengths, owners)
-    gathered, select = lax.optimization_barrier((gathered, select))
-    partial, sent = project(snapshots, gathered, 256)
+    partial, sent = project(snapshots, gathered, 2)
     swap = [(i, i ^ 1) for i in range(devices)]
     other = lax.ppermute(sent, "space", swap)
     packed = call(

time: 81.9 us -> 79.6 us (0.972)
  blocking collectives: 44.2 us -> 68.3 us
  waiting for transfers between devices: 17.5 us -> 1.13 us
  starting transfers between devices: 8.97 us -> 1.92 us
  Pallas kernels: 8.94 us -> 6.11 us
    all_to_all x0 -> x1, blocking collectives: none -> 24 us  [on_device(): gathered = lax.all_to_all(copies, 'tm', 0, 0, tiled=True)]
    all_to_all x1 -> x0, waiting for transfers between devices: 15.6 us -> none  [on_device(): lax.all_to_all(spread(basis, groups_tm), 'tm', 0, 0, tiled=True)]
    all_to_all x1 -> x0, starting transfers between devices: 7.05 us -> none  [on_device(): lax.all_to_all(spread(basis, groups_tm), 'tm', 0, 0, tiled=True)]
    pallas_call x2 -> x1, Pallas kernels: 6.07 us -> 3.25 us  [project(): pl.pallas_call(project_kernel, grid=(steps,), out_shape=tuple((jax.ShapeD...]
    unnamed x6, local copies, waits for them, and re-layouts: 1.31 us -> 0.02 us
    transpose x0 -> x1, local copies, waits for them, and re-layouts: none -> 0.95 us  [on_device(): copies = jnp.broadcast_to(basis.T[None], (groups_tm, modes, basis.shape[0]))]
  transfers between devices with their start and end apart: 2 -> 1, of which waited for: 2 -> 1; matrix products, arithmetic and copies ran while one was open for 0% -> 0% of each run, Pallas kernels for 1% -> 1%
where the time goes in v4:
time: 79.6 us; the launch traced here: 79.4 us
  blocking collectives  68.3 us (86%)
  Pallas kernels  6.11 us (8%)
  starting transfers between devices  1.92 us (2%)
  local copies, waits for them, and re-layouts  1.16 us (1%)
  waiting for transfers between devices  1.13 us (1%)
    all_to_all x1, blocking collectives, on_device(): lax.all_to_all(packed.reshape(chips, SLOTS, -1), 'space', 0, 0, axis_inde...  44.3 us
    all_to_all x1, blocking collectives, on_device(): gathered = lax.all_to_all(copies, 'tm', 0, 0, tiled=True)  24 us
    pallas_call x1, Pallas kernels, project(): pl.pallas_call(project_kernel, grid=(steps,), out_shape=tuple((jax.ShapeD...  3.25 us
    ppermute x1, starting transfers between devices, on_device(): other = lax.ppermute(sent, 'space', swap)  1.92 us
  transfers between devices with their start and end apart: 1, of which 1 were waited for; matrix products, arithmetic and copies ran while one was open for 0% of the time, Pallas kernels for 1%

profile of v4, /device:TPU:32, one launch (start us, length us, event | category | flops | bytes accessed | tf_op | source)
XLA Modules:
  0.0 79.4 jit_solution(468148120245803925)
XLA Ops:
  0.6 0.9 %copy.7 = bf16[256,128]{1,0:T(8,128)(2,1)S(1)} copy(bf16[256,128]{0,1:T(8,128)(2,1)} %bitcast.6) | data formatting | bytes 131072 | tf_op jit(solution)/shard_map/transpose | solution.py:155
  1.6 0.0 copy-start.1
  1.6 0.0 copy-start.2
  1.6 0.2 broadcast_in_dim.12
  1.8 24.0 %all_to_all.10.basis_ref = bf16[16,256,128]{2,1,0:T(8,128)(2,1)S(1)} all-to-all(bf16[16,256,128]{2,1,0:T(8,128)(2,1)S(1)} %broadcast_in_dim.12), channel_id=1, replica_groups=mesh['space'=32,'tm'=16] {'tm'}, dimensions={0} | all-to-all | bytes 2097152 | tf_op jit(solution)/shard_map/all_to_all | solution.py:156
  25.8 0.0 copy-start
  25.8 3.2 %project.1 = (f32[256,1024]{1,0:T(8,128)S(1)}, bf16[256,1024]{1,0:T(8,128)(2,1)S(1)}) custom-call(bf16[2048,1024]{1,0:T(8,128)(2,1)} %snapshots_ref.1, bf16[16,256,128]{2,1,0:T(8,128)(2,1)S(1)} %all_to_all.10.basis_ref), custom_call_target="tpu_custom_call" | custom-call | flops 1073741824 | bytes 4194304 | tf_op jit(solution)/shard_map/project/pallas_call | solution.py:77
  29.1 1.9 %collective-permute-start = (bf16[256,1024]{1,0:T(8,128)(2,1)S(1)}, bf16[256,1024]{1,0:T(8,128)(2,1)S(1)}, u32[]{:S(2)}, u32[]{:S(2)}) collective-permute-start(bf16[256,1024]{1,0:T(8,128)(2,1)S(1)} %get-tuple-element.10), channel_id=1, source_target_pairs={{0,16},{16,0},{32,48},{48,32},{64,80},{80,64},{96,112},{112,96},{1... | collective-permute-start | bytes 1572872 | tf_op jit(solution)/shard_map/ppermute | solution.py:167
  31.0 0.0 copy-done.1
  31.0 0.0 copy-done.2
  31.0 0.7 prepare.1
  31.7 1.1 %collective-permute-done.other_ref = bf16[256,1024]{1,0:T(8,128)(2,1)S(1)} collective-permute-done((bf16[256,1024]{1,0:T(8,128)(2,1)S(1)}, bf16[256,1024]{1,0:T(8,128)(2,1)S(1)}, u32[]{:S(2)}, u32[]{:S(2)}) %collective-permute-start) | collective-permute-done | bytes 524320 | tf_op jit(solution)/shard_map/ppermute | solution.py:167
  32.9 0.8 pack.1
  33.6 44.3 %all_to_all.11.refs_0_ = bf16[16,64,256]{2,1,0:T(8,128)(2,1)S(1)} all-to-all(bf16[16,64,256]{2,1,0:T(8,128)(2,1)S(1)} %bitcast.5), channel_id=1, replica_groups={{0,32,64,96,128,160,192,224,256,288,320,352,384,416,448,480},{16,48,80,..., dimensions={0} | all-to-all | bytes 1048576 | tf_op jit(solution)/shard_map/all_to_all | solution.py:177
  78.0 0.0 copy-done
  78.0 1.4 %library.1 = (bf16[392,392]{1,0:T(8,128)(2,1)}, bf16[392,256]{1,0:T(8,128)(2,1)}) custom-call(bf16[16,64,256]{2,1,0:T(8,128)(2,1)S(1)} %all_to_all.11.refs_0_, f32[64,128]{1,0:T(8,128)S(1)} %get-tuple-element.11.refs_1_, f32[128,512]{1,0:T(8,128)S(1)} %copy-done), custom_call_target="tpu_custom_call" | custom-call | flops 32514048 | bytes 508032 | tf_op jit(solution)/shard_map/library/pallas_call | solution.py:182
Async XLA Ops:
  1.6 29.4 %copy-start.1 = (s32[1,64]{1,0:T(1,128)S(1)}, s32[1,64]{1,0:T(1,128)}, u32[]{:S(2)}) copy-start(s32[1,64]{1,0:T(1,128)} %length_ref.1) | copy-start | bytes 772
  1.6 29.4 %copy-start.2 = (s32[1,64]{1,0:T(1,128)S(1)}, s32[1,64]{1,0:T(1,128)}, u32[]{:S(2)}) copy-start(s32[1,64]{1,0:T(1,128)} %owner_ref.1) | copy-start | bytes 772
  25.8 52.2 %copy-start = (f32[128,512]{1,0:T(8,128)S(1)}, f32[128,512]{1,0:T(8,128)}, u32[]{:S(2)}) copy-start(f32[128,512]{1,0:T(8,128)} %constant.8.clone.refs_2_) | copy-start | bytes 786436
  29.1 3.8 %collective-permute-start = (bf16[256,1024]{1,0:T(8,128)(2,1)S(1)}, bf16[256,1024]{1,0:T(8,128)(2,1)S(1)}, u32[]{:S(2)}, u32[]{:S(2)}) collective-permute-start(bf16[256,1024]{1,0:T(8,128)(2,1)S(1)} %get-tuple-element.10), channel_id=1, source_target_pairs={{0,16},{16,0},{32,48},{48,32},{64,80},{80,64},{96,112},{112,96},{1... | collective-permute-start | bytes 1572872 | tf_op jit(solution)/shard_map/ppermute | solution.py:167

commit v5 on v4

--- a/solution.py
+++ b/solution.py
@@ -9,11 +9,17 @@
 QM = 16
 SLOTS = 64
 LANES = 128
+FIRST_PAIR = 4
+FIRST_TM = 10
 f32 = jnp.float32
 bf16 = jnp.bfloat16
 i32 = jnp.int32
 VMEM = pl.BlockSpec(memory_space=pltpu.VMEM)
 SMEM = pl.BlockSpec(memory_space=pltpu.SMEM)
+
+
+def rotated(pair, count):
+    return jnp.bitwise_and(pair - FIRST_PAIR, count - 1)
 
 
 def iota(shape, axis):
@@ -32,9 +38,13 @@
     same = owner_row == owner_col
     starts = jnp.sum(jnp.where(tj < ti, length_row, 0), axis=1, keepdims=True)
     offset = jnp.sum(jnp.where((tj < ti) & same, length_row, 0), axis=1, keepdims=True)
+    chip = jnp.right_shift(owner_col, 1)
+    across = jnp.bitwise_and(chip + jnp.right_shift(own, 1), 1)
+    half = select_ref.shape[0] // (2 * SLOTS)
+    place = across * half + rotated(jnp.right_shift(chip, 1), half)
     base = jnp.where(
         jnp.bitwise_and(owner_col, 1) == jnp.bitwise_and(own, 1),
-        jnp.right_shift(owner_col, 1) * SLOTS + offset - starts,
+        place * SLOTS + offset - starts,
         -2 * snap_count,
     )
     snap = iota((t, snap_count), 1)
@@ -55,9 +65,12 @@
 
 
 def project_kernel(snapshots_ref, basis_ref, partial_ref, sent_ref):
-    left = jnp.concatenate([basis_ref[i] for i in range(basis_ref.shape[0])], axis=1)
+    step = pl.program_id(0)
+    blocks, _, width = basis_ref.shape
+    count = snapshots_ref.shape[0] // width
+    turn = [jnp.bitwise_and(step * count + i - FIRST_TM, blocks - 1) for i in range(count)]
+    left = jnp.concatenate([basis_ref[i] for i in turn], axis=1)
     piece = jnp.dot(left, snapshots_ref[...], preferred_element_type=f32)
-    step = pl.program_id(0)
 
     @pl.when(step == 0)
     def _():
@@ -67,22 +80,24 @@
     def _():
         total = partial_ref[...] + piece
         partial_ref[...] = total
-        sent_ref[...] = total.astype(bf16)
+        high = total.astype(bf16)
+        sent_ref[: total.shape[0], :] = high
+        sent_ref[total.shape[0] :, :] = (total[:QM] - high[:QM].astype(f32)).astype(bf16)
 
 
 def project(snapshots, basis, steps):
     cells, snap_count = snapshots.shape
-    blocks, modes, width = basis.shape
-    whole = pl.BlockSpec((modes, snap_count), lambda i: (0, 0))
+    modes = basis.shape[1]
+    heights = (modes, modes + QM)
     return pl.pallas_call(
         project_kernel,
         grid=(steps,),
-        out_shape=tuple(jax.ShapeDtypeStruct((modes, snap_count), kind) for kind in (f32, bf16)),
+        out_shape=tuple(jax.ShapeDtypeStruct((h, snap_count), kind) for h, kind in zip(heights, (f32, bf16))),
         in_specs=[
             pl.BlockSpec((cells // steps, snap_count), lambda i: (i, 0)),
-            pl.BlockSpec((blocks // steps, modes, width), lambda i: (i, 0, 0)),
+            VMEM,
         ],
-        out_specs=(whole, whole),
+        out_specs=tuple(pl.BlockSpec((h, snap_count), lambda i: (0, 0)) for h in heights),
         compiler_params=pltpu.CompilerParams(vmem_limit_bytes=50 << 20),
         cost_estimate=pl.CostEstimate(
             flops=2 * cells * snap_count * modes, bytes_accessed=2 * cells * snap_count, transcendentals=0
@@ -91,17 +106,46 @@
     )(snapshots, basis)
 
 
-def pack_kernel(select_ref, partial_ref, other_ref, packed_ref):
-    chip_sum = (partial_ref[...] + other_ref[...].astype(f32)).astype(bf16)
-    step = 256
-    for at in range(0, select_ref.shape[0], step):
-        packed_ref[pl.ds(at, step), :] = lax.dot_general(
-            select_ref[pl.ds(at, step), :], chip_sum, (((1,), (1,)), ((), ())), preferred_element_type=f32
-        ).astype(bf16)
-
-
-def library_kernel(weight_scale, parts_ref, live_ref, pick_ref, gram_ref, target_ref):
-    coords = jnp.sum(parts_ref[...].astype(f32), axis=0)
+NT = (((1,), (1,)), ((), ()))
+
+
+def chip_sum(partial_ref, other_ref):
+    modes = partial_ref.shape[0]
+    total = partial_ref[...] + other_ref[:modes].astype(f32)
+    lead = total[:QM] + other_ref[modes:].astype(f32)
+    total = jnp.concatenate([lead, total[QM:]], axis=0)
+    high = total.astype(bf16)
+    return high, (total - high.astype(f32)).astype(bf16)
+
+
+def give_kernel(select_ref, partial_ref, other_ref, given_ref):
+    high, _ = chip_sum(partial_ref, other_ref)
+    count = given_ref.shape[0]
+    given_ref[...] = lax.dot_general(
+        select_ref[count:, :], high, NT, preferred_element_type=f32
+    ).astype(bf16)
+
+
+def keep_kernel(select_ref, partial_ref, other_ref, kept_ref):
+    high, low = chip_sum(partial_ref, other_ref)
+    select = select_ref[: kept_ref.shape[0], :]
+    kept_ref[...] = lax.dot_general(select, high, NT, preferred_element_type=f32) + lax.dot_general(
+        select, low, NT, preferred_element_type=f32
+    )
+
+
+def merge_kernel(own_ref, kept_ref, given_ref, merged_ref, mine_ref):
+    merged_ref[...] = (kept_ref[...] + given_ref[...].astype(f32)).astype(bf16)
+    me = rotated(jnp.right_shift(own_ref[0], 2), kept_ref.shape[0] // SLOTS)
+    at = pl.ds(pl.multiple_of(me * SLOTS, SLOTS), SLOTS)
+    mine_ref[...] = kept_ref[at, :] + given_ref[at, :].astype(f32)
+
+
+def library_kernel(weight_scale, own_ref, parts_ref, mine_ref, live_ref, pick_ref, gram_ref, target_ref):
+    me = rotated(jnp.right_shift(own_ref[0], 2), parts_ref.shape[0])
+    coords = mine_ref[...]
+    for i in range(parts_ref.shape[0]):
+        coords = coords + jnp.where(i == me, 0.0, parts_ref[i].astype(f32))
     modes = coords.shape[1]
     terms = pick_ref.shape[1] // 2
     both = jnp.dot(
@@ -153,7 +197,8 @@
     shape = jax.ShapeDtypeStruct
 
     copies = jnp.broadcast_to(basis.T[None], (groups_tm, modes, basis.shape[0]))
-    gathered = lax.all_to_all(copies, "tm", 0, 0, tiled=True)
+    order = [(i + FIRST_TM) % groups_tm for i in range(groups_tm)]
+    gathered = lax.all_to_all(copies, "tm", 0, 0, axis_index_groups=[order], tiled=True)
     select, live = call(
         prepare_kernel,
         "prepare",
@@ -165,17 +210,30 @@
     partial, sent = project(snapshots, gathered, 2)
     swap = [(i, i ^ 1) for i in range(devices)]
     other = lax.ppermute(sent, "space", swap)
-    packed = call(
-        pack_kernel,
-        "pack",
-        shape((rows, modes), bf16),
-        [VMEM, VMEM, VMEM],
-        2 * rows * snap_count * modes,
-        6 * snap_count * modes,
+    kept_rows = rows // 2
+    flops = rows * snap_count * modes
+    given = call(
+        give_kernel, "give", shape((kept_rows, modes), bf16), [VMEM] * 3, flops, 4 * rows * modes
     )(select, partial, other)
-    along_z = [[2 * z + c for z in range(chips)] for c in range(2)]
+    near = [(2 * z, 2 * (z ^ 1)) for z in range(chips)]
+    near += [(2 * z + 1, 2 * ((((z + 1) ^ 1) - 1) % chips) + 1) for z in range(chips)]
+    given = lax.ppermute(given, "space", near)
+    kept = call(
+        keep_kernel, "keep", shape((kept_rows, modes), f32), [VMEM] * 3, 2 * flops, 4 * rows * modes
+    )(select, partial, other)
+    merged, mine = call(
+        merge_kernel,
+        "merge",
+        (shape((kept_rows, modes), bf16), shape((SLOTS, modes), f32)),
+        [SMEM, VMEM, VMEM],
+        rows * modes,
+        4 * rows * modes,
+    )(own.reshape(1), kept, given)
+    pairs = chips // 2
+    order = [(i + FIRST_PAIR) % pairs for i in range(pairs)]
+    along_z = [[2 * (2 * pair + p) + c for pair in order] for p in range(2) for c in range(2)]
     parts = lax.all_to_all(
-        packed.reshape(chips, SLOTS, -1), "space", 0, 0, axis_index_groups=along_z, tiled=True
+        merged.reshape(pairs, SLOTS, -1), "space", 0, 0, axis_index_groups=along_z, tiled=True
     )
     term_count, table = picks()
     terms = modes + term_count
@@ -183,10 +241,10 @@
         lambda *refs: library_kernel(devices / snap_count, *refs),
         "library",
         (shape((terms, terms), bf16), shape((terms, modes), bf16)),
-        [VMEM, VMEM, VMEM],
+        [SMEM] + [VMEM] * 4,
         2 * SLOTS * terms * (terms + modes),
         2 * terms * (terms + modes),
-    )(parts, live, jnp.asarray(table))
+    )(own.reshape(1), parts, mine, live, jnp.asarray(table))
     return gram[None, None], target[None, None]
 
 

time: 79.6 us -> 71.5 us (0.90)
  the two profiles are of different devices: /device:TPU:32 before, /device:TPU:1 now
where the time goes in v5:
time: 71.5 us; the launch traced here: 71.2 us
  blocking collectives  41.8 us (58%)
  starting transfers between devices  17.1 us (24%)
  Pallas kernels  6.61 us (9%)
  waiting for transfers between devices  3.79 us (5%)
  local copies, waits for them, and re-layouts  1.16 us (2%)
  between operations  0.73 us (1%)
    all_to_all x1, blocking collectives, on_device(): lax.all_to_all(merged.reshape(pairs, SLOTS, -1), 'space', 0, 0, axis_inde...  23.6 us
    all_to_all x1, blocking collectives, on_device(): lax.all_to_all(copies, 'tm', 0, 0, axis_index_groups=[order], tiled=True)  18.2 us
    ppermute x1, starting transfers between devices, on_device(): given = lax.ppermute(given, 'space', near)  11 us
    ppermute x1, starting transfers between devices, on_device(): other = lax.ppermute(sent, 'space', swap)  6.15 us
    pallas_call x1, Pallas kernels, project(): pl.pallas_call(project_kernel, grid=(steps,), out_shape=tuple((jax.ShapeD...  3.21 us
    ppermute x1, waiting for transfers between devices, on_device(): given = lax.ppermute(given, 'space', near)  2.98 us
  transfers between devices with their start and end apart: 2, of which 2 were waited for; matrix products, arithmetic and copies ran while one was open for 0% of the time, Pallas kernels for 2%

profile of v5, /device:TPU:1, one launch (start us, length us, event | category | flops | bytes accessed | tf_op | source)
XLA Modules:
  0.0 71.2 jit_solution(16925354890470697555)
XLA Ops:
  0.6 0.9 %copy.7 = bf16[256,128]{1,0:T(8,128)(2,1)S(1)} copy(bf16[256,128]{0,1:T(8,128)(2,1)} %bitcast.6) | data formatting | bytes 131072 | tf_op jit(solution)/shard_map/transpose | solution.py:199
  1.6 0.0 copy-start.1
  1.6 0.0 copy-start.2
  1.6 0.2 broadcast_in_dim.12
  1.8 18.2 %all_to_all.10.basis_ref = bf16[16,256,128]{2,1,0:T(8,128)(2,1)S(1)} all-to-all(bf16[16,256,128]{2,1,0:T(8,128)(2,1)S(1)} %broadcast_in_dim.12), channel_id=1, replica_groups={{10,11,12,13,14,15,0,1,2,3,4,5,6,7,8,9},{26,27,28,29,30,31,16,17,18,19,..., dimensions={0} | all-to-all | bytes 2097152 | tf_op jit(solution)/shard_map/all_to_all | solution.py:201
  20.0 3.2 %project.1 = (f32[256,1024]{1,0:T(8,128)S(1)}, bf16[272,1024]{1,0:T(8,128)(2,1)S(1)}) custom-call(bf16[2048,1024]{1,0:T(8,128)(2,1)} %snapshots_ref.1, bf16[16,256,128]{2,1,0:T(8,128)(2,1)S(1)} %all_to_all.10.basis_ref), custom_call_target="tpu_custom_call" | custom-call | flops 1073741824 | bytes 4194304 | tf_op jit(solution)/shard_map/project/pallas_call | solution.py:92
  23.2 6.2 %collective-permute-start = (bf16[272,1024]{1,0:T(8,128)(2,1)S(1)}, bf16[272,1024]{1,0:T(8,128)(2,1)S(1)}, u32[]{:S(2)}, u32[]{:S(2)}) collective-permute-start(bf16[272,1024]{1,0:T(8,128)(2,1)S(1)} %get-tuple-element.12), channel_id=1, source_target_pairs={{0,16},{16,0},{32,48},{48,32},{64,80},{80,64},{96,112},{112,96},{1... | collective-permute-start | bytes 1671176 | tf_op jit(solution)/shard_map/ppermute | solution.py:212
  29.4 0.0 copy-done.1
  29.4 0.0 copy-done.2
  29.4 0.7 %prepare.1 = (bf16[1024,1024]{1,0:T(8,128)(2,1)S(1)}, f32[64,128]{1,0:T(8,128)S(1)}) custom-call(s32[1]{0:T(128)} %bitcast.own_ref.refs_0_, s32[1,64]{1,0:T(1,128)S(1)} %copy-done.1, s32[1,64]{1,0:T(1,128)S(1)} %copy-done.2), custom_call_target="tpu_custom_call" | custom-call | flops 4194304 | bytes 2097152 | tf_op jit(solution)/shard_map/prepare/pallas_call | solution.py:202
  30.1 0.8 %collective-permute-done.other_ref = bf16[272,1024]{1,0:T(8,128)(2,1)S(1)} collective-permute-done((bf16[272,1024]{1,0:T(8,128)(2,1)S(1)}, bf16[272,1024]{1,0:T(8,128)(2,1)S(1)}, u32[]{:S(2)}, u32[]{:S(2)}) %collective-permute-start) | collective-permute-done | bytes 557088 | tf_op jit(solution)/shard_map/ppermute | solution.py:212
  30.9 0.0 copy-start
  30.9 0.5 give.1
  31.4 11.0 %collective-permute-start.1 = (bf16[512,256]{1,0:T(8,128)(2,1)S(1)}, bf16[512,256]{1,0:T(8,128)(2,1)S(1)}, u32[]{:S(2)}, u32[]{:S(2)}) collective-permute-start(bf16[512,256]{1,0:T(8,128)(2,1)S(1)} %give.1), channel_id=1, source_target_pairs={{0,32},{32,0},{64,96},{96,64},{128,160},{160,128},{192,224},{224,1... | collective-permute-start | bytes 786440 | tf_op jit(solution)/shard_map/ppermute | solution.py:220
  42.4 0.8 %keep.1.kept_ref = f32[512,256]{1,0:T(8,128)S(1)} custom-call(bf16[1024,1024]{1,0:T(8,128)(2,1)S(1)} %get-tuple-element.10.select_ref, f32[256,1024]{1,0:T(8,128)S(1)} %get-tuple-element.11.partial_ref, bf16[272,1024]{1,0:T(8,128)(2,1)S(1)} %collective-permute-done.other_ref), custom_call_target="tpu_custom_call" | custom-call | flops 536870912 | bytes 1048576 | tf_op jit(solution)/shard_map/keep/pallas_call | solution.py:221
  43.2 3.0 %collective-permute-done.1.given_ref = bf16[512,256]{1,0:T(8,128)(2,1)S(1)} collective-permute-done((bf16[512,256]{1,0:T(8,128)(2,1)S(1)}, bf16[512,256]{1,0:T(8,128)(2,1)S(1)}, u32[]{:S(2)}, u32[]{:S(2)}) %collective-permute-start.1) | collective-permute-done | bytes 262176 | tf_op jit(solution)/shard_map/ppermute | solution.py:220
  46.2 0.1 merge.1
  46.2 23.6 %all_to_all.11.refs_1_ = bf16[8,64,256]{2,1,0:T(8,128)(2,1)S(1)} all-to-all(bf16[8,64,256]{2,1,0:T(8,128)(2,1)S(1)} %bitcast.5), channel_id=1, replica_groups={{256,320,384,448,0,64,128,192},{272,336,400,464,16,80,144,208},{288,352..., dimensions={0} | all-to-all | bytes 524288 | tf_op jit(solution)/shard_map/all_to_all | solution.py:235
  69.8 0.0 copy-done
  69.8 1.4 %library.1 = (bf16[392,392]{1,0:T(8,128)(2,1)}, bf16[392,256]{1,0:T(8,128)(2,1)}) custom-call(s32[1]{0:T(128)} %bitcast.own_ref.refs_0_, bf16[8,64,256]{2,1,0:T(8,128)(2,1)S(1)} %all_to_all.11.refs_1_, f32[64,256]{1,0:T(8,128)S(1)} %get-tuple-element.14.refs_2_, f32[64,128]{1,0:T(8,128)S(1)} %get-tuple-element.15.refs_3_, f32[128,512]{1,0:T(8,128)S(1)} %copy-done), custom_call_target="tpu_custom_call" | custom-call | flops 32514048 | bytes 508032 | tf_op jit(solution)/shard_map/library/pallas_call | solution.py:240
Async XLA Ops:
  1.6 27.8 %copy-start.1 = (s32[1,64]{1,0:T(1,128)S(1)}, s32[1,64]{1,0:T(1,128)}, u32[]{:S(2)}) copy-start(s32[1,64]{1,0:T(1,128)} %length_ref.1) | copy-start | bytes 772
  1.6 27.8 %copy-start.2 = (s32[1,64]{1,0:T(1,128)S(1)}, s32[1,64]{1,0:T(1,128)}, u32[]{:S(2)}) copy-start(s32[1,64]{1,0:T(1,128)} %owner_ref.1) | copy-start | bytes 772
  23.2 7.7 %collective-permute-start = (bf16[272,1024]{1,0:T(8,128)(2,1)S(1)}, bf16[272,1024]{1,0:T(8,128)(2,1)S(1)}, u32[]{:S(2)}, u32[]{:S(2)}) collective-permute-start(bf16[272,1024]{1,0:T(8,128)(2,1)S(1)} %get-tuple-element.12), channel_id=1, source_target_pairs={{0,16},{16,0},{32,48},{48,32},{64,80},{80,64},{96,112},{112,96},{1... | collective-permute-start | bytes 1671176 | tf_op jit(solution)/shard_map/ppermute | solution.py:212
  30.9 38.9 %copy-start = (f32[128,512]{1,0:T(8,128)S(1)}, f32[128,512]{1,0:T(8,128)}, u32[]{:S(2)}) copy-start(f32[128,512]{1,0:T(8,128)} %constant.8.clone.refs_4_) | copy-start | bytes 786436
  31.4 14.7 %collective-permute-start.1 = (bf16[512,256]{1,0:T(8,128)(2,1)S(1)}, bf16[512,256]{1,0:T(8,128)(2,1)S(1)}, u32[]{:S(2)}, u32[]{:S(2)}) collective-permute-start(bf16[512,256]{1,0:T(8,128)(2,1)S(1)} %give.1), channel_id=1, source_target_pairs={{0,32},{32,0},{64,96},{96,64},{128,160},{160,128},{192,224},{224,1... | collective-permute-start | bytes 786440 | tf_op jit(solution)/shard_map/ppermute | solution.py:220

commit v6 on v5

--- a/solution.py
+++ b/solution.py
@@ -66,11 +66,13 @@
 
 def project_kernel(snapshots_ref, basis_ref, partial_ref, sent_ref):
     step = pl.program_id(0)
-    blocks, _, width = basis_ref.shape
+    blocks, width, modes = basis_ref.shape
     count = snapshots_ref.shape[0] // width
     turn = [jnp.bitwise_and(step * count + i - FIRST_TM, blocks - 1) for i in range(count)]
-    left = jnp.concatenate([basis_ref[i] for i in turn], axis=1)
-    piece = jnp.dot(left, snapshots_ref[...], preferred_element_type=f32)
+    basis = jnp.concatenate([basis_ref[i] for i in turn], axis=0)
+    piece = lax.dot_general(
+        basis, snapshots_ref[...], (((0,), (0,)), ((), ())), preferred_element_type=f32
+    )
 
     @pl.when(step == 0)
     def _():
@@ -87,7 +89,7 @@
 
 def project(snapshots, basis, steps):
     cells, snap_count = snapshots.shape
-    modes = basis.shape[1]
+    modes = basis.shape[2]
     heights = (modes, modes + QM)
     return pl.pallas_call(
         project_kernel,
@@ -196,7 +198,7 @@
     rows = chips * SLOTS
     shape = jax.ShapeDtypeStruct
 
-    copies = jnp.broadcast_to(basis.T[None], (groups_tm, modes, basis.shape[0]))
+    copies = jnp.broadcast_to(basis[None], (groups_tm,) + basis.shape)
     order = [(i + FIRST_TM) % groups_tm for i in range(groups_tm)]
     gathered = lax.all_to_all(copies, "tm", 0, 0, axis_index_groups=[order], tiled=True)
     select, live = call(
@@ -215,8 +217,8 @@
     given = call(
         give_kernel, "give", shape((kept_rows, modes), bf16), [VMEM] * 3, flops, 4 * rows * modes
     )(select, partial, other)
-    near = [(2 * z, 2 * (z ^ 1)) for z in range(chips)]
-    near += [(2 * z + 1, 2 * ((((z + 1) ^ 1) - 1) % chips) + 1) for z in range(chips)]
+    near = [(2 * z + 1, 2 * (z ^ 1) + 1) for z in range(chips)]
+    near += [(2 * z, 2 * ((((z + 1) ^ 1) - 1) % chips)) for z in range(chips)]
     given = lax.ppermute(given, "space", near)
     kept = call(
         keep_kernel, "keep", shape((kept_rows, modes), f32), [VMEM] * 3, 2 * flops, 4 * rows * modes

time: 71.5 us -> 69 us (0.965)
  the two profiles are of different devices: /device:TPU:1 before, /device:TPU:4 now
where the time goes in v6:
time: 69 us; the launch traced here: 68.7 us
  blocking collectives  42.4 us (61%)
  starting transfers between devices  13.3 us (19%)
  Pallas kernels  6.68 us (10%)
  waiting for transfers between devices  4.73 us (7%)
  local copies, waits for them, and re-layouts  0.96 us (1%)
  between operations  0.73 us (1%)
    all_to_all x1, blocking collectives, on_device(): lax.all_to_all(merged.reshape(pairs, SLOTS, -1), 'space', 0, 0, axis_inde...  21.5 us
    all_to_all x1, blocking collectives, on_device(): lax.all_to_all(copies, 'tm', 0, 0, axis_index_groups=[order], tiled=True)  20.8 us
    ppermute x1, starting transfers between devices, on_device(): given = lax.ppermute(given, 'space', near)  11.4 us
    ppermute x1, waiting for transfers between devices, on_device(): given = lax.ppermute(given, 'space', near)  3.57 us
    pallas_call x1, Pallas kernels, project(): pl.pallas_call(project_kernel, grid=(steps,), out_shape=tuple((jax.ShapeD...  3.28 us
    ppermute x1, starting transfers between devices, on_device(): other = lax.ppermute(sent, 'space', swap)  1.92 us
    pallas_call x1, Pallas kernels, on_device(): call(lambda *refs: library_kernel(devices / snap_count, *refs), 'library'...  1.39 us
  transfers between devices with their start and end apart: 2, of which 2 were waited for; matrix products, arithmetic and copies ran while one was open for 0% of the time, Pallas kernels for 2%

profile of v6, /device:TPU:4, one launch (start us, length us, event | category | flops | bytes accessed | tf_op | source)
XLA Modules:
  0.0 68.7 jit_solution(12961226479872669714)
XLA Ops:
  0.6 0.0 copy-start.2
  0.6 0.0 copy-start.1
  0.7 0.9 %broadcast_in_dim.12 = bf16[16,128,256]{2,1,0:T(8,128)(2,1)S(1)} broadcast(bf16[128,256]{1,0:T(8,128)(2,1)} %param.6), dimensions={1,2} | broadcast | bytes 1114112 | tf_op jit(solution)/shard_map/broadcast_in_dim | solution.py:201
  1.6 20.8 %all_to_all.10.basis_ref = bf16[16,128,256]{2,1,0:T(8,128)(2,1)S(1)} all-to-all(bf16[16,128,256]{2,1,0:T(8,128)(2,1)S(1)} %broadcast_in_dim.12), channel_id=1, replica_groups={{10,11,12,13,14,15,0,1,2,3,4,5,6,7,8,9},{26,27,28,29,30,31,16,17,18,19,..., dimensions={0} | all-to-all | bytes 2097152 | tf_op jit(solution)/shard_map/all_to_all | solution.py:203
  22.4 3.3 %project.1 = (f32[256,1024]{1,0:T(8,128)S(1)}, bf16[272,1024]{1,0:T(8,128)(2,1)S(1)}) custom-call(bf16[2048,1024]{1,0:T(8,128)(2,1)} %snapshots_ref.1, bf16[16,128,256]{2,1,0:T(8,128)(2,1)S(1)} %all_to_all.10.basis_ref), custom_call_target="tpu_custom_call" | custom-call | flops 1073741824 | bytes 4194304 | tf_op jit(solution)/shard_map/project/pallas_call | solution.py:94
  25.7 1.9 %collective-permute-start = (bf16[272,1024]{1,0:T(8,128)(2,1)S(1)}, bf16[272,1024]{1,0:T(8,128)(2,1)S(1)}, u32[]{:S(2)}, u32[]{:S(2)}) collective-permute-start(bf16[272,1024]{1,0:T(8,128)(2,1)S(1)} %get-tuple-element.12), channel_id=1, source_target_pairs={{0,16},{16,0},{32,48},{48,32},{64,80},{80,64},{96,112},{112,96},{1... | collective-permute-start | bytes 1671176 | tf_op jit(solution)/shard_map/ppermute | solution.py:214
  27.6 0.0 copy-done.2
  27.6 0.0 copy-done.1
  27.7 0.7 %prepare.1 = (bf16[1024,1024]{1,0:T(8,128)(2,1)S(1)}, f32[64,128]{1,0:T(8,128)S(1)}) custom-call(s32[1]{0:T(128)} %bitcast.own_ref.refs_0_, s32[1,64]{1,0:T(1,128)S(1)} %copy-done.1, s32[1,64]{1,0:T(1,128)S(1)} %copy-done.2), custom_call_target="tpu_custom_call" | custom-call | flops 4194304 | bytes 2097152 | tf_op jit(solution)/shard_map/prepare/pallas_call | solution.py:204
  28.4 1.2 %collective-permute-done.other_ref = bf16[272,1024]{1,0:T(8,128)(2,1)S(1)} collective-permute-done((bf16[272,1024]{1,0:T(8,128)(2,1)S(1)}, bf16[272,1024]{1,0:T(8,128)(2,1)S(1)}, u32[]{:S(2)}, u32[]{:S(2)}) %collective-permute-start) | collective-permute-done | bytes 557088 | tf_op jit(solution)/shard_map/ppermute | solution.py:214
  29.5 0.0 copy-start
  29.6 0.5 give.1
  30.0 11.4 %collective-permute-start.1 = (bf16[512,256]{1,0:T(8,128)(2,1)S(1)}, bf16[512,256]{1,0:T(8,128)(2,1)S(1)}, u32[]{:S(2)}, u32[]{:S(2)}) collective-permute-start(bf16[512,256]{1,0:T(8,128)(2,1)S(1)} %give.1), channel_id=1, source_target_pairs={{16,48},{48,16},{80,112},{112,80},{144,176},{176,144},{208,240},{2... | collective-permute-start | bytes 786440 | tf_op jit(solution)/shard_map/ppermute | solution.py:222
  41.4 0.8 %keep.1.kept_ref = f32[512,256]{1,0:T(8,128)S(1)} custom-call(bf16[1024,1024]{1,0:T(8,128)(2,1)S(1)} %get-tuple-element.10.select_ref, f32[256,1024]{1,0:T(8,128)S(1)} %get-tuple-element.11.partial_ref, bf16[272,1024]{1,0:T(8,128)(2,1)S(1)} %collective-permute-done.other_ref), custom_call_target="tpu_custom_call" | custom-call | flops 536870912 | bytes 1048576 | tf_op jit(solution)/shard_map/keep/pallas_call | solution.py:223
  42.2 3.6 %collective-permute-done.1.given_ref = bf16[512,256]{1,0:T(8,128)(2,1)S(1)} collective-permute-done((bf16[512,256]{1,0:T(8,128)(2,1)S(1)}, bf16[512,256]{1,0:T(8,128)(2,1)S(1)}, u32[]{:S(2)}, u32[]{:S(2)}) %collective-permute-start.1) | collective-permute-done | bytes 262176 | tf_op jit(solution)/shard_map/ppermute | solution.py:222
  45.7 0.1 merge.1
  45.8 21.5 %all_to_all.11.refs_1_ = bf16[8,64,256]{2,1,0:T(8,128)(2,1)S(1)} all-to-all(bf16[8,64,256]{2,1,0:T(8,128)(2,1)S(1)} %bitcast.4), channel_id=1, replica_groups={{256,320,384,448,0,64,128,192},{272,336,400,464,16,80,144,208},{288,352..., dimensions={0} | all-to-all | bytes 524288 | tf_op jit(solution)/shard_map/all_to_all | solution.py:237
  67.3 0.0 copy-done
  67.3 1.4 %library.1 = (bf16[392,392]{1,0:T(8,128)(2,1)}, bf16[392,256]{1,0:T(8,128)(2,1)}) custom-call(s32[1]{0:T(128)} %bitcast.own_ref.refs_0_, bf16[8,64,256]{2,1,0:T(8,128)(2,1)S(1)} %all_to_all.11.refs_1_, f32[64,256]{1,0:T(8,128)S(1)} %get-tuple-element.14.refs_2_, f32[64,128]{1,0:T(8,128)S(1)} %get-tuple-element.15.refs_3_, f32[128,512]{1,0:T(8,128)S(1)} %copy-done), custom_call_target="tpu_custom_call" | custom-call | flops 32514048 | bytes 508032 | tf_op jit(solution)/shard_map/library/pallas_call | solution.py:242
Async XLA Ops:
  0.6 27.0 %copy-start.2 = (s32[1,64]{1,0:T(1,128)S(1)}, s32[1,64]{1,0:T(1,128)}, u32[]{:S(2)}) copy-start(s32[1,64]{1,0:T(1,128)} %owner_ref.1) | copy-start | bytes 772
  0.6 27.0 %copy-start.1 = (s32[1,64]{1,0:T(1,128)S(1)}, s32[1,64]{1,0:T(1,128)}, u32[]{:S(2)}) copy-start(s32[1,64]{1,0:T(1,128)} %length_ref.1) | copy-start | bytes 772
  25.7 3.9 %collective-permute-start = (bf16[272,1024]{1,0:T(8,128)(2,1)S(1)}, bf16[272,1024]{1,0:T(8,128)(2,1)S(1)}, u32[]{:S(2)}, u32[]{:S(2)}) collective-permute-start(bf16[272,1024]{1,0:T(8,128)(2,1)S(1)} %get-tuple-element.12), channel_id=1, source_target_pairs={{0,16},{16,0},{32,48},{48,32},{64,80},{80,64},{96,112},{112,96},{1... | collective-permute-start | bytes 1671176 | tf_op jit(solution)/shard_map/ppermute | solution.py:214
  29.5 37.8 %copy-start = (f32[128,512]{1,0:T(8,128)S(1)}, f32[128,512]{1,0:T(8,128)}, u32[]{:S(2)}) copy-start(f32[128,512]{1,0:T(8,128)} %constant.8.clone.refs_4_) | copy-start | bytes 786436
  30.0 15.7 %collective-permute-start.1 = (bf16[512,256]{1,0:T(8,128)(2,1)S(1)}, bf16[512,256]{1,0:T(8,128)(2,1)S(1)}, u32[]{:S(2)}, u32[]{:S(2)}) collective-permute-start(bf16[512,256]{1,0:T(8,128)(2,1)S(1)} %give.1), channel_id=1, source_target_pairs={{16,48},{48,16},{80,112},{112,80},{144,176},{176,144},{208,240},{2... | collective-permute-start | bytes 786440 | tf_op jit(solution)/shard_map/ppermute | solution.py:222

commit v7 on v6

--- a/solution.py
+++ b/solution.py
@@ -9,7 +9,7 @@
 QM = 16
 SLOTS = 64
 LANES = 128
-FIRST_PAIR = 4
+FIRST_PAIR = (6, 5)
 FIRST_TM = 10
 f32 = jnp.float32
 bf16 = jnp.bfloat16
@@ -18,8 +18,9 @@
 SMEM = pl.BlockSpec(memory_space=pltpu.SMEM)
 
 
-def rotated(pair, count):
-    return jnp.bitwise_and(pair - FIRST_PAIR, count - 1)
+def rotated(chip, count):
+    first = jnp.where(jnp.bitwise_and(chip, 1) == 0, FIRST_PAIR[0], FIRST_PAIR[1])
+    return jnp.bitwise_and(jnp.right_shift(chip, 1) - first, count - 1)
 
 
 def iota(shape, axis):
@@ -41,7 +42,7 @@
     chip = jnp.right_shift(owner_col, 1)
     across = jnp.bitwise_and(chip + jnp.right_shift(own, 1), 1)
     half = select_ref.shape[0] // (2 * SLOTS)
-    place = across * half + rotated(jnp.right_shift(chip, 1), half)
+    place = across * half + rotated(chip, half)
     base = jnp.where(
         jnp.bitwise_and(owner_col, 1) == jnp.bitwise_and(own, 1),
         place * SLOTS + offset - starts,
@@ -138,13 +139,13 @@
 
 def merge_kernel(own_ref, kept_ref, given_ref, merged_ref, mine_ref):
     merged_ref[...] = (kept_ref[...] + given_ref[...].astype(f32)).astype(bf16)
-    me = rotated(jnp.right_shift(own_ref[0], 2), kept_ref.shape[0] // SLOTS)
+    me = rotated(jnp.right_shift(own_ref[0], 1), kept_ref.shape[0] // SLOTS)
     at = pl.ds(pl.multiple_of(me * SLOTS, SLOTS), SLOTS)
     mine_ref[...] = kept_ref[at, :] + given_ref[at, :].astype(f32)
 
 
 def library_kernel(weight_scale, own_ref, parts_ref, mine_ref, live_ref, pick_ref, gram_ref, target_ref):
-    me = rotated(jnp.right_shift(own_ref[0], 2), parts_ref.shape[0])
+    me = rotated(jnp.right_shift(own_ref[0], 1), parts_ref.shape[0])
     coords = mine_ref[...]
     for i in range(parts_ref.shape[0]):
         coords = coords + jnp.where(i == me, 0.0, parts_ref[i].astype(f32))
@@ -232,8 +233,8 @@
         4 * rows * modes,
     )(own.reshape(1), kept, given)
     pairs = chips // 2
-    order = [(i + FIRST_PAIR) % pairs for i in range(pairs)]
-    along_z = [[2 * (2 * pair + p) + c for pair in order] for p in range(2) for c in range(2)]
+    order = [[(i + first) % pairs for i in range(pairs)] for first in FIRST_PAIR]
+    along_z = [[2 * (2 * pair + p) + c for pair in order[p]] for p in range(2) for c in range(2)]
     parts = lax.all_to_all(
         merged.reshape(pairs, SLOTS, -1), "space", 0, 0, axis_index_groups=along_z, tiled=True
     )

time: 69 us -> 68.9 us (level)
  no operation moved by 1% of the time
where the time goes in v7:
time: 68.9 us; the launch traced here: 68.6 us
  blocking collectives  42.2 us (61%)
  starting transfers between devices  13.3 us (19%)
  Pallas kernels  6.68 us (10%)
  waiting for transfers between devices  4.74 us (7%)
  local copies, waits for them, and re-layouts  0.96 us (1%)
  between operations  0.73 us (1%)
    all_to_all x1, blocking collectives, on_device(): lax.all_to_all(merged.reshape(pairs, SLOTS, -1), 'space', 0, 0, axis_inde...  21.4 us
    all_to_all x1, blocking collectives, on_device(): lax.all_to_all(copies, 'tm', 0, 0, axis_index_groups=[order], tiled=True)  20.8 us
    ppermute x1, starting transfers between devices, on_device(): given = lax.ppermute(given, 'space', near)  11.4 us
    ppermute x1, waiting for transfers between devices, on_device(): given = lax.ppermute(given, 'space', near)  3.57 us
    pallas_call x1, Pallas kernels, project(): pl.pallas_call(project_kernel, grid=(steps,), out_shape=tuple((jax.ShapeD...  3.28 us
    ppermute x1, starting transfers between devices, on_device(): other = lax.ppermute(sent, 'space', swap)  1.92 us
    pallas_call x1, Pallas kernels, on_device(): call(lambda *refs: library_kernel(devices / snap_count, *refs), 'library'...  1.39 us
  transfers between devices with their start and end apart: 2, of which 2 were waited for; matrix products, arithmetic and copies ran while one was open for 0% of the time, Pallas kernels for 2%

profile of v7, /device:TPU:4, one launch (start us, length us, event | category | flops | bytes accessed | tf_op | source)
XLA Modules:
  0.0 68.6 jit_solution(15384733953907755234)
XLA Ops:
  0.6 0.0 copy-start.2
  0.6 0.0 copy-start.1
  0.7 0.9 %broadcast_in_dim.12 = bf16[16,128,256]{2,1,0:T(8,128)(2,1)S(1)} broadcast(bf16[128,256]{1,0:T(8,128)(2,1)} %param.6), dimensions={1,2} | broadcast | bytes 1114112 | tf_op jit(solution)/shard_map/broadcast_in_dim | solution.py:202
  1.6 20.8 %all_to_all.10.basis_ref = bf16[16,128,256]{2,1,0:T(8,128)(2,1)S(1)} all-to-all(bf16[16,128,256]{2,1,0:T(8,128)(2,1)S(1)} %broadcast_in_dim.12), channel_id=1, replica_groups={{10,11,12,13,14,15,0,1,2,3,4,5,6,7,8,9},{26,27,28,29,30,31,16,17,18,19,..., dimensions={0} | all-to-all | bytes 2097152 | tf_op jit(solution)/shard_map/all_to_all | solution.py:204
  22.4 3.3 %project.1 = (f32[256,1024]{1,0:T(8,128)S(1)}, bf16[272,1024]{1,0:T(8,128)(2,1)S(1)}) custom-call(bf16[2048,1024]{1,0:T(8,128)(2,1)} %snapshots_ref.1, bf16[16,128,256]{2,1,0:T(8,128)(2,1)S(1)} %all_to_all.10.basis_ref), custom_call_target="tpu_custom_call" | custom-call | flops 1073741824 | bytes 4194304 | tf_op jit(solution)/shard_map/project/pallas_call | solution.py:95
  25.7 1.9 %collective-permute-start = (bf16[272,1024]{1,0:T(8,128)(2,1)S(1)}, bf16[272,1024]{1,0:T(8,128)(2,1)S(1)}, u32[]{:S(2)}, u32[]{:S(2)}) collective-permute-start(bf16[272,1024]{1,0:T(8,128)(2,1)S(1)} %get-tuple-element.12), channel_id=1, source_target_pairs={{0,16},{16,0},{32,48},{48,32},{64,80},{80,64},{96,112},{112,96},{1... | collective-permute-start | bytes 1671176 | tf_op jit(solution)/shard_map/ppermute | solution.py:215
  27.6 0.0 copy-done.2
  27.6 0.0 copy-done.1
  27.7 0.7 %prepare.1 = (bf16[1024,1024]{1,0:T(8,128)(2,1)S(1)}, f32[64,128]{1,0:T(8,128)S(1)}) custom-call(s32[1]{0:T(128)} %bitcast.own_ref.refs_0_, s32[1,64]{1,0:T(1,128)S(1)} %copy-done.1, s32[1,64]{1,0:T(1,128)S(1)} %copy-done.2), custom_call_target="tpu_custom_call" | custom-call | flops 4194304 | bytes 2097152 | tf_op jit(solution)/shard_map/prepare/pallas_call | solution.py:205
  28.4 1.2 %collective-permute-done.other_ref = bf16[272,1024]{1,0:T(8,128)(2,1)S(1)} collective-permute-done((bf16[272,1024]{1,0:T(8,128)(2,1)S(1)}, bf16[272,1024]{1,0:T(8,128)(2,1)S(1)}, u32[]{:S(2)}, u32[]{:S(2)}) %collective-permute-start) | collective-permute-done | bytes 557088 | tf_op jit(solution)/shard_map/ppermute | solution.py:215
  29.5 0.0 copy-start
  29.6 0.5 give.1
  30.0 11.4 %collective-permute-start.1 = (bf16[512,256]{1,0:T(8,128)(2,1)S(1)}, bf16[512,256]{1,0:T(8,128)(2,1)S(1)}, u32[]{:S(2)}, u32[]{:S(2)}) collective-permute-start(bf16[512,256]{1,0:T(8,128)(2,1)S(1)} %give.1), channel_id=1, source_target_pairs={{16,48},{48,16},{80,112},{112,80},{144,176},{176,144},{208,240},{2... | collective-permute-start | bytes 786440 | tf_op jit(solution)/shard_map/ppermute | solution.py:223
  41.4 0.8 %keep.1.kept_ref = f32[512,256]{1,0:T(8,128)S(1)} custom-call(bf16[1024,1024]{1,0:T(8,128)(2,1)S(1)} %get-tuple-element.10.select_ref, f32[256,1024]{1,0:T(8,128)S(1)} %get-tuple-element.11.partial_ref, bf16[272,1024]{1,0:T(8,128)(2,1)S(1)} %collective-permute-done.other_ref), custom_call_target="tpu_custom_call" | custom-call | flops 536870912 | bytes 1048576 | tf_op jit(solution)/shard_map/keep/pallas_call | solution.py:224
  42.2 3.6 %collective-permute-done.1.given_ref = bf16[512,256]{1,0:T(8,128)(2,1)S(1)} collective-permute-done((bf16[512,256]{1,0:T(8,128)(2,1)S(1)}, bf16[512,256]{1,0:T(8,128)(2,1)S(1)}, u32[]{:S(2)}, u32[]{:S(2)}) %collective-permute-start.1) | collective-permute-done | bytes 262176 | tf_op jit(solution)/shard_map/ppermute | solution.py:223
  45.7 0.1 merge.1
  45.8 21.4 %all_to_all.11.refs_1_ = bf16[8,64,256]{2,1,0:T(8,128)(2,1)S(1)} all-to-all(bf16[8,64,256]{2,1,0:T(8,128)(2,1)S(1)} %bitcast.4), channel_id=1, replica_groups={{384,448,0,64,128,192,256,320},{400,464,16,80,144,208,272,336},{352,416..., dimensions={0} | all-to-all | bytes 524288 | tf_op jit(solution)/shard_map/all_to_all | solution.py:238
  67.2 0.0 copy-done
  67.2 1.4 %library.1 = (bf16[392,392]{1,0:T(8,128)(2,1)}, bf16[392,256]{1,0:T(8,128)(2,1)}) custom-call(s32[1]{0:T(128)} %bitcast.own_ref.refs_0_, bf16[8,64,256]{2,1,0:T(8,128)(2,1)S(1)} %all_to_all.11.refs_1_, f32[64,256]{1,0:T(8,128)S(1)} %get-tuple-element.14.refs_2_, f32[64,128]{1,0:T(8,128)S(1)} %get-tuple-element.15.refs_3_, f32[128,512]{1,0:T(8,128)S(1)} %copy-done), custom_call_target="tpu_custom_call" | custom-call | flops 32514048 | bytes 508032 | tf_op jit(solution)/shard_map/library/pallas_call | solution.py:243
Async XLA Ops:
  0.6 27.0 %copy-start.2 = (s32[1,64]{1,0:T(1,128)S(1)}, s32[1,64]{1,0:T(1,128)}, u32[]{:S(2)}) copy-start(s32[1,64]{1,0:T(1,128)} %owner_ref.1) | copy-start | bytes 772
  0.6 27.0 %copy-start.1 = (s32[1,64]{1,0:T(1,128)S(1)}, s32[1,64]{1,0:T(1,128)}, u32[]{:S(2)}) copy-start(s32[1,64]{1,0:T(1,128)} %length_ref.1) | copy-start | bytes 772
  25.7 3.9 %collective-permute-start = (bf16[272,1024]{1,0:T(8,128)(2,1)S(1)}, bf16[272,1024]{1,0:T(8,128)(2,1)S(1)}, u32[]{:S(2)}, u32[]{:S(2)}) collective-permute-start(bf16[272,1024]{1,0:T(8,128)(2,1)S(1)} %get-tuple-element.12), channel_id=1, source_target_pairs={{0,16},{16,0},{32,48},{48,32},{64,80},{80,64},{96,112},{112,96},{1... | collective-permute-start | bytes 1671176 | tf_op jit(solution)/shard_map/ppermute | solution.py:215
  29.5 37.7 %copy-start = (f32[128,512]{1,0:T(8,128)S(1)}, f32[128,512]{1,0:T(8,128)}, u32[]{:S(2)}) copy-start(f32[128,512]{1,0:T(8,128)} %constant.8.clone.refs_4_) | copy-start | bytes 786436
  30.0 15.7 %collective-permute-start.1 = (bf16[512,256]{1,0:T(8,128)(2,1)S(1)}, bf16[512,256]{1,0:T(8,128)(2,1)S(1)}, u32[]{:S(2)}, u32[]{:S(2)}) collective-permute-start(bf16[512,256]{1,0:T(8,128)(2,1)S(1)} %give.1), channel_id=1, source_target_pairs={{16,48},{48,16},{80,112},{112,80},{144,176},{176,144},{208,240},{2... | collective-permute-start | bytes 786440 | tf_op jit(solution)/shard_map/ppermute | solution.py:223
